TPU v7x, 256 devices: a whole 4x4x8 slice. The times are simulated.
256 devices in a mesh: col: 16 (over z, core), sec: 16 (over y, x).
Axes of the slice: x: 4, y: 4, z: 8, core: 2. Of those that a mesh axis runs over, the one named last changes fastest.
Arguments:
- env_right: bfloat16 [1, 65536, 128], P(None, 'sec'), may hold values from -6 to 6
- transfer: bfloat16 [16, 1, 65536, 4, 128], P('col', None, 'sec'), may hold values from -0.25 to 0.25
- sources: int32 [16, 1, 512, 4], P('col', None, 'sec'), may hold values from 0 to 511, as said below
- env_left: bfloat16 [16, 1, 65536, 128], P('col', None, 'sec'), may hold values from -0.5 to 0.5
Outputs:
- env_out: bfloat16 [16, 1, 65536, 128], P('col', None, 'sec')
- grad: bfloat16 [16, 1, 65536, 4, 128], P('col', None, 'sec')
Inputs may be any that keep to these rules, and one draw needn't show every extreme that they name: `sources`: every source tile lies within 2 tiles of its output tile; each list holds the tiles at offsets -2 and +2 (reflected at the ends of the space) and two of the offsets -1, 0, 1.
All inputs are finite; a program needn't handle non-finite values.
Results may differ from a plain program's by a relative error of at most 0.029.
Values may be sent and summed in bfloat16 or wider, within the bound.
A program may use at most 64 MiB of HBM per device.

v0:
```python
import jax
import jax.numpy as jnp
from jax import lax
from jax.sharding import PartitionSpec as P

TILE = 128
REACH = 2


def passed_along(value, axis, by):
    devices = lax.axis_size(axis)
    pairs = [(i, i + by) for i in range(devices) if 0 <= i + by < devices]
    return lax.ppermute(value, axis, pairs)


def padded(value, sides, width):
    for axis, dim in sides:
        devices, length = (lax.axis_size(axis), value.shape[dim])
        up = [(i, (i + 1) % devices) for i in range(devices - 1)]
        down = [(j, i) for i, j in up]
        last = lax.slice_in_dim(value, length - width, length, axis=dim)
        leading = lax.slice_in_dim(value, 0, width, axis=dim)
        before = lax.ppermute(last, axis, up)
        after = lax.ppermute(leading, axis, down)
        value = jnp.concatenate([before, value, after], axis=dim)
    return value


def pick_blocks(haloed, local_sources):
    batch = haloed.shape[0]
    width = haloed.shape[2]
    blocks = haloed.reshape(batch, -1, TILE, width)

    def one_row(row_blocks, row_sources):
        return row_blocks[row_sources]

    return jax.vmap(one_row)(blocks, local_sources)


def advance(block_rows, picked):
    batch = block_rows.shape[0]
    length = block_rows.shape[1]
    tiles_here = length // TILE
    blocks = block_rows.reshape(batch, tiles_here, TILE, block_rows.shape[2], block_rows.shape[3])
    fresh = jnp.einsum("rtopq,rtpqk->rtok", blocks, picked, preferred_element_type=jnp.float32)
    return fresh.reshape(batch, length, picked.shape[-1]).astype(jnp.bfloat16)


def gradient(left_rows, picked, pairs, tile_width):
    batch = left_rows.shape[0]
    length = left_rows.shape[1]
    width = left_rows.shape[2]
    left = left_rows.reshape(batch, length // TILE, TILE, width)
    block_grad = jnp.einsum("rtok,rtpqk->rtopq", left, picked, preferred_element_type=jnp.float32)
    return block_grad.reshape(batch, length, pairs, tile_width).astype(jnp.bfloat16)


def per_device(env_right, transfer, sources, env_left):
    ncol = lax.axis_size("col")
    col_index = lax.axis_index("col")
    sec_index = lax.axis_index("sec")
    rows = transfer.shape[1]
    length = transfer.shape[2]
    pairs = transfer.shape[3]
    tile_width = transfer.shape[4]
    tiles_here = length // TILE
    width = env_right.shape[2]
    is_last = col_index == ncol - 1
    block_rows = transfer[0]
    local_sources = sources[0] - sec_index * tiles_here + REACH
    picked_shape = (rows, tiles_here, pairs, TILE, width)

    def step(turn, carry):
        state, picked = carry
        received = passed_along(state, "col", -1)
        received = jnp.where(is_last, env_right, received)
        haloed = padded(received, (("sec", 1),), REACH * TILE)
        picked = pick_blocks(haloed, local_sources)
        return (advance(block_rows, picked), picked)

    start_state = jnp.zeros_like(env_right)
    start_picked = jnp.zeros(picked_shape, jnp.bfloat16)
    env_final, picked_final = lax.fori_loop(0, ncol, step, (start_state, start_picked))
    grad = gradient(env_left[0], picked_final, pairs, tile_width)
    return (env_final[None], grad[None])


def solution(mesh):
    placed = (
        P(None, "sec", None),
        P("col", None, "sec", None, None),
        P("col", None, "sec", None),
        P("col", None, "sec", None),
    )
    return jax.shard_map(
        per_device,
        mesh=mesh,
        in_specs=placed,
        out_specs=(P("col", None, "sec", None), P("col", None, "sec", None, None)),
        check_vma=False,
    )
```

profile of v0, /device:TPU:121, one launch (start us, length us, event | category | flops | bytes accessed | tf_op | source)
XLA Modules:
  0.0 582.2 jit_solution(5522162164011241718)
XLA Ops:
  2.7 554.9 %while.12 = (s32[]{:T(128)}, bf16[1,4096,128]{2,1,0:T(8,128)(2,1)S(1)}, bf16[1,32,4,128,128]{4,3,2,1,0:T(8,128)(2,1)}, pred[]{:T(512)}, bf16[1,4096,128]{2,1,0:T...) while((s32[]{:T(128)}, bf16[1,4096,128]{2,1,0:T(8,128)(2,1)S(1)}, ...), condition=%wide.region_1.2_spmd, body=%wide.region_0.1_spmd.sunk | while | flops 541459456 | bytes 28318924 | solution.py:83
  5.3 15.2 %collective-permute-done = bf16[1,4096,128]{2,1,0:T(8,128)(2,1)S(1)} collective-permute-done((bf16[1,4096,128]{2,1,0:T(8,128)(2,1)S(1)}, bf16[1,4096,128]{2,1,0:T(8,128)(2,1)S(1)}, u32[]{:S(2)}, u32[]{:S(2)}) %collective-permute-start) | collective-permute-done | bytes 1048608 | tf_op jit(solution)/shard_map/while/body/eval_jaxpr/ppermute | solution.py:13
  20.7 4.6 collective-permute-start.1
  27.4 5.0 collective-permute-done.2
  35.6 4.7 bitcast_convert_fusion.2
  42.2 15.4 %collective-permute-done = bf16[1,4096,128]{2,1,0:T(8,128)(2,1)S(1)} collective-permute-done((bf16[1,4096,128]{2,1,0:T(8,128)(2,1)S(1)}, bf16[1,4096,128]{2,1,0:T(8,128)(2,1)S(1)}, u32[]{:S(2)}, u32[]{:S(2)}) %collective-permute-start) | collective-permute-done | bytes 1048608 | tf_op jit(solution)/shard_map/while/body/eval_jaxpr/ppermute | solution.py:13
  63.3 3.5 collective-permute-done.2
  70.1 4.7 bitcast_convert_fusion.2
  76.7 15.4 %collective-permute-done = bf16[1,4096,128]{2,1,0:T(8,128)(2,1)S(1)} collective-permute-done((bf16[1,4096,128]{2,1,0:T(8,128)(2,1)S(1)}, bf16[1,4096,128]{2,1,0:T(8,128)(2,1)S(1)}, u32[]{:S(2)}, u32[]{:S(2)}) %collective-permute-start) | collective-permute-done | bytes 1048608 | tf_op jit(solution)/shard_map/while/body/eval_jaxpr/ppermute | solution.py:13
  97.8 3.5 collective-permute-done.2
  104.5 4.7 bitcast_convert_fusion.2
  111.2 15.4 %collective-permute-done = bf16[1,4096,128]{2,1,0:T(8,128)(2,1)S(1)} collective-permute-done((bf16[1,4096,128]{2,1,0:T(8,128)(2,1)S(1)}, bf16[1,4096,128]{2,1,0:T(8,128)(2,1)S(1)}, u32[]{:S(2)}, u32[]{:S(2)}) %collective-permute-start) | collective-permute-done | bytes 1048608 | tf_op jit(solution)/shard_map/while/body/eval_jaxpr/ppermute | solution.py:13
  132.3 3.5 collective-permute-done.2
  139.0 4.7 bitcast_convert_fusion.2
  145.7 15.4 %collective-permute-done = bf16[1,4096,128]{2,1,0:T(8,128)(2,1)S(1)} collective-permute-done((bf16[1,4096,128]{2,1,0:T(8,128)(2,1)S(1)}, bf16[1,4096,128]{2,1,0:T(8,128)(2,1)S(1)}, u32[]{:S(2)}, u32[]{:S(2)}) %collective-permute-start) | collective-permute-done | bytes 1048608 | tf_op jit(solution)/shard_map/while/body/eval_jaxpr/ppermute | solution.py:13
  166.8 3.5 collective-permute-done.2
  173.5 4.7 bitcast_convert_fusion.2
  180.2 15.4 %collective-permute-done = bf16[1,4096,128]{2,1,0:T(8,128)(2,1)S(1)} collective-permute-done((bf16[1,4096,128]{2,1,0:T(8,128)(2,1)S(1)}, bf16[1,4096,128]{2,1,0:T(8,128)(2,1)S(1)}, u32[]{:S(2)}, u32[]{:S(2)}) %collective-permute-start) | collective-permute-done | bytes 1048608 | tf_op jit(solution)/shard_map/while/body/eval_jaxpr/ppermute | solution.py:13
  201.3 3.5 collective-permute-done.2
  208.0 4.7 bitcast_convert_fusion.2
  214.7 15.4 %collective-permute-done = bf16[1,4096,128]{2,1,0:T(8,128)(2,1)S(1)} collective-permute-done((bf16[1,4096,128]{2,1,0:T(8,128)(2,1)S(1)}, bf16[1,4096,128]{2,1,0:T(8,128)(2,1)S(1)}, u32[]{:S(2)}, u32[]{:S(2)}) %collective-permute-start) | collective-permute-done | bytes 1048608 | tf_op jit(solution)/shard_map/while/body/eval_jaxpr/ppermute | solution.py:13
  235.8 3.5 collective-permute-done.2
  242.5 4.7 bitcast_convert_fusion.2
  249.2 15.4 %collective-permute-done = bf16[1,4096,128]{2,1,0:T(8,128)(2,1)S(1)} collective-permute-done((bf16[1,4096,128]{2,1,0:T(8,128)(2,1)S(1)}, bf16[1,4096,128]{2,1,0:T(8,128)(2,1)S(1)}, u32[]{:S(2)}, u32[]{:S(2)}) %collective-permute-start) | collective-permute-done | bytes 1048608 | tf_op jit(solution)/shard_map/while/body/eval_jaxpr/ppermute | solution.py:13
  270.2 3.5 collective-permute-done.2
  277.0 4.7 bitcast_convert_fusion.2
  283.6 15.4 %collective-permute-done = bf16[1,4096,128]{2,1,0:T(8,128)(2,1)S(1)} collective-permute-done((bf16[1,4096,128]{2,1,0:T(8,128)(2,1)S(1)}, bf16[1,4096,128]{2,1,0:T(8,128)(2,1)S(1)}, u32[]{:S(2)}, u32[]{:S(2)}) %collective-permute-start) | collective-permute-done | bytes 1048608 | tf_op jit(solution)/shard_map/while/body/eval_jaxpr/ppermute | solution.py:13
  304.7 3.5 collective-permute-done.2
  311.4 4.7 bitcast_convert_fusion.2
  318.1 15.4 %collective-permute-done = bf16[1,4096,128]{2,1,0:T(8,128)(2,1)S(1)} collective-permute-done((bf16[1,4096,128]{2,1,0:T(8,128)(2,1)S(1)}, bf16[1,4096,128]{2,1,0:T(8,128)(2,1)S(1)}, u32[]{:S(2)}, u32[]{:S(2)}) %collective-permute-start) | collective-permute-done | bytes 1048608 | tf_op jit(solution)/shard_map/while/body/eval_jaxpr/ppermute | solution.py:13
  339.2 3.5 collective-permute-done.2
  345.9 4.7 bitcast_convert_fusion.2
  352.6 15.4 %collective-permute-done = bf16[1,4096,128]{2,1,0:T(8,128)(2,1)S(1)} collective-permute-done((bf16[1,4096,128]{2,1,0:T(8,128)(2,1)S(1)}, bf16[1,4096,128]{2,1,0:T(8,128)(2,1)S(1)}, u32[]{:S(2)}, u32[]{:S(2)}) %collective-permute-start) | collective-permute-done | bytes 1048608 | tf_op jit(solution)/shard_map/while/body/eval_jaxpr/ppermute | solution.py:13
  373.7 3.5 collective-permute-done.2
  380.4 4.7 bitcast_convert_fusion.2
  387.1 15.4 %collective-permute-done = bf16[1,4096,128]{2,1,0:T(8,128)(2,1)S(1)} collective-permute-done((bf16[1,4096,128]{2,1,0:T(8,128)(2,1)S(1)}, bf16[1,4096,128]{2,1,0:T(8,128)(2,1)S(1)}, u32[]{:S(2)}, u32[]{:S(2)}) %collective-permute-start) | collective-permute-done | bytes 1048608 | tf_op jit(solution)/shard_map/while/body/eval_jaxpr/ppermute | solution.py:13
  414.9 4.7 bitcast_convert_fusion.2
  421.6 15.4 %collective-permute-done = bf16[1,4096,128]{2,1,0:T(8,128)(2,1)S(1)} collective-permute-done((bf16[1,4096,128]{2,1,0:T(8,128)(2,1)S(1)}, bf16[1,4096,128]{2,1,0:T(8,128)(2,1)S(1)}, u32[]{:S(2)}, u32[]{:S(2)}) %collective-permute-start) | collective-permute-done | bytes 1048608 | tf_op jit(solution)/shard_map/while/body/eval_jaxpr/ppermute | solution.py:13
  449.4 4.7 bitcast_convert_fusion.2
  456.1 15.4 %collective-permute-done = bf16[1,4096,128]{2,1,0:T(8,128)(2,1)S(1)} collective-permute-done((bf16[1,4096,128]{2,1,0:T(8,128)(2,1)S(1)}, bf16[1,4096,128]{2,1,0:T(8,128)(2,1)S(1)}, u32[]{:S(2)}, u32[]{:S(2)}) %collective-permute-start) | collective-permute-done | bytes 1048608 | tf_op jit(solution)/shard_map/while/body/eval_jaxpr/ppermute | solution.py:13
  483.9 4.7 bitcast_convert_fusion.2
  490.5 15.4 %collective-permute-done = bf16[1,4096,128]{2,1,0:T(8,128)(2,1)S(1)} collective-permute-done((bf16[1,4096,128]{2,1,0:T(8,128)(2,1)S(1)}, bf16[1,4096,128]{2,1,0:T(8,128)(2,1)S(1)}, u32[]{:S(2)}, u32[]{:S(2)}) %collective-permute-start) | collective-permute-done | bytes 1048608 | tf_op jit(solution)/shard_map/while/body/eval_jaxpr/ppermute | solution.py:13
  511.6 3.5 collective-permute-done.2
  518.3 4.7 bitcast_convert_fusion.2
  525.0 15.4 %collective-permute-done = bf16[1,4096,128]{2,1,0:T(8,128)(2,1)S(1)} collective-permute-done((bf16[1,4096,128]{2,1,0:T(8,128)(2,1)S(1)}, bf16[1,4096,128]{2,1,0:T(8,128)(2,1)S(1)}, u32[]{:S(2)}, u32[]{:S(2)}) %collective-permute-start) | collective-permute-done | bytes 1048608 | tf_op jit(solution)/shard_map/while/body/eval_jaxpr/ppermute | solution.py:13
  552.8 4.7 bitcast_convert_fusion.2
  557.6 3.8 convert_bitcast_fusion
  561.7 20.4 %copy.11 = bf16[1,1,4096,4,128]{4,3,2,1,0:T(4,128)(2,1)} copy(bf16[1,1,4096,4,128]{4,2,3,1,0:T(8,128)(2,1)S(1)} %bitcast.54) | data formatting | bytes 8388608
  (219 shorter events, 186.2 us)
Async XLA Ops:
  2.7 17.8 %collective-permute-start = (bf16[1,4096,128]{2,1,0:T(8,128)(2,1)S(1)}, bf16[1,4096,128]{2,1,0:T(8,128)(2,1)S(1)}, u32[]{:S(2)}, u32[]{:S(2)}) collective-permute-start(bf16[1,4096,128]{2,1,0:T(8,128)(2,1)S(1)} %get-tuple-element.113), channel_id=1, source_target_pairs={{16,0},{32,16},{48,32},{64,48},{80,64},{96,80},{112,96},{128,112},... | collective-permute-start | bytes 3145736 | tf_op jit(solution)/shard_map/while/body/eval_jaxpr/ppermute | solution.py:13
  20.7 6.7 %collective-permute-start.1 = (bf16[1,256,128]{2,1,0:T(8,128)(2,1)S(1)}, bf16[1,256,128]{2,1,0:T(8,128)(2,1)S(1)}, u32[]{:S(2)}, u32[]{:S(2)}) collective-permute-start(bf16[1,256,128]{2,1,0:T(8,128)(2,1)S(1)} %get-tuple-element.102), channel_id=1, source_target_pairs={{1,0},{2,1},{3,2},{4,3},{5,4},{6,5},{7,6},{8,7},{9,8},{10,9},{11,1... | collective-permute-start | bytes 196616 | tf_op jit(solution)/shard_map/while/body/eval_jaxpr/ppermute | solution.py:24
  25.3 7.1 %collective-permute-start.2 = (bf16[1,256,128]{2,1,0:T(8,128)(2,1)S(1)}, bf16[1,256,128]{2,1,0:T(8,128)(2,1)S(1)}, u32[]{:S(2)}, u32[]{:S(2)}) collective-permute-start(bf16[1,256,128]{2,1,0:T(8,128)(2,1)S(1)} %get-tuple-element.103), channel_id=1, source_target_pairs={{0,1},{1,2},{2,3},{3,4},{4,5},{5,6},{6,7},{7,8},{8,9},{9,10},{10,1... | collective-permute-start | bytes 196616 | tf_op jit(solution)/shard_map/while/body/eval_jaxpr/ppermute | solution.py:23
  40.3 17.3 %collective-permute-start = (bf16[1,4096,128]{2,1,0:T(8,128)(2,1)S(1)}, bf16[1,4096,128]{2,1,0:T(8,128)(2,1)S(1)}, u32[]{:S(2)}, u32[]{:S(2)}) collective-permute-start(bf16[1,4096,128]{2,1,0:T(8,128)(2,1)S(1)} %get-tuple-element.113), channel_id=1, source_target_pairs={{16,0},{32,16},{48,32},{64,48},{80,64},{96,80},{112,96},{128,112},... | collective-permute-start | bytes 3145736 | tf_op jit(solution)/shard_map/while/body/eval_jaxpr/ppermute | solution.py:13
  57.8 5.5 collective-permute-start.1
  59.7 7.1 %collective-permute-start.2 = (bf16[1,256,128]{2,1,0:T(8,128)(2,1)S(1)}, bf16[1,256,128]{2,1,0:T(8,128)(2,1)S(1)}, u32[]{:S(2)}, u32[]{:S(2)}) collective-permute-start(bf16[1,256,128]{2,1,0:T(8,128)(2,1)S(1)} %get-tuple-element.103), channel_id=1, source_target_pairs={{0,1},{1,2},{2,3},{3,4},{4,5},{5,6},{6,7},{7,8},{8,9},{9,10},{10,1... | collective-permute-start | bytes 196616 | tf_op jit(solution)/shard_map/while/body/eval_jaxpr/ppermute | solution.py:23
  74.8 17.3 %collective-permute-start = (bf16[1,4096,128]{2,1,0:T(8,128)(2,1)S(1)}, bf16[1,4096,128]{2,1,0:T(8,128)(2,1)S(1)}, u32[]{:S(2)}, u32[]{:S(2)}) collective-permute-start(bf16[1,4096,128]{2,1,0:T(8,128)(2,1)S(1)} %get-tuple-element.113), channel_id=1, source_target_pairs={{16,0},{32,16},{48,32},{64,48},{80,64},{96,80},{112,96},{128,112},... | collective-permute-start | bytes 3145736 | tf_op jit(solution)/shard_map/while/body/eval_jaxpr/ppermute | solution.py:13
  92.3 5.5 collective-permute-start.1
  94.2 7.1 %collective-permute-start.2 = (bf16[1,256,128]{2,1,0:T(8,128)(2,1)S(1)}, bf16[1,256,128]{2,1,0:T(8,128)(2,1)S(1)}, u32[]{:S(2)}, u32[]{:S(2)}) collective-permute-start(bf16[1,256,128]{2,1,0:T(8,128)(2,1)S(1)} %get-tuple-element.103), channel_id=1, source_target_pairs={{0,1},{1,2},{2,3},{3,4},{4,5},{5,6},{6,7},{7,8},{8,9},{9,10},{10,1... | collective-permute-start | bytes 196616 | tf_op jit(solution)/shard_map/while/body/eval_jaxpr/ppermute | solution.py:23
  109.3 17.3 %collective-permute-start = (bf16[1,4096,128]{2,1,0:T(8,128)(2,1)S(1)}, bf16[1,4096,128]{2,1,0:T(8,128)(2,1)S(1)}, u32[]{:S(2)}, u32[]{:S(2)}) collective-permute-start(bf16[1,4096,128]{2,1,0:T(8,128)(2,1)S(1)} %get-tuple-element.113), channel_id=1, source_target_pairs={{16,0},{32,16},{48,32},{64,48},{80,64},{96,80},{112,96},{128,112},... | collective-permute-start | bytes 3145736 | tf_op jit(solution)/shard_map/while/body/eval_jaxpr/ppermute | solution.py:13
  126.8 5.5 collective-permute-start.1
  128.7 7.1 %collective-permute-start.2 = (bf16[1,256,128]{2,1,0:T(8,128)(2,1)S(1)}, bf16[1,256,128]{2,1,0:T(8,128)(2,1)S(1)}, u32[]{:S(2)}, u32[]{:S(2)}) collective-permute-start(bf16[1,256,128]{2,1,0:T(8,128)(2,1)S(1)} %get-tuple-element.103), channel_id=1, source_target_pairs={{0,1},{1,2},{2,3},{3,4},{4,5},{5,6},{6,7},{7,8},{8,9},{9,10},{10,1... | collective-permute-start | bytes 196616 | tf_op jit(solution)/shard_map/while/body/eval_jaxpr/ppermute | solution.py:23
  143.7 17.3 %collective-permute-start = (bf16[1,4096,128]{2,1,0:T(8,128)(2,1)S(1)}, bf16[1,4096,128]{2,1,0:T(8,128)(2,1)S(1)}, u32[]{:S(2)}, u32[]{:S(2)}) collective-permute-start(bf16[1,4096,128]{2,1,0:T(8,128)(2,1)S(1)} %get-tuple-element.113), channel_id=1, source_target_pairs={{16,0},{32,16},{48,32},{64,48},{80,64},{96,80},{112,96},{128,112},... | collective-permute-start | bytes 3145736 | tf_op jit(solution)/shard_map/while/body/eval_jaxpr/ppermute | solution.py:13
  161.3 5.5 collective-permute-start.1
  163.2 7.1 %collective-permute-start.2 = (bf16[1,256,128]{2,1,0:T(8,128)(2,1)S(1)}, bf16[1,256,128]{2,1,0:T(8,128)(2,1)S(1)}, u32[]{:S(2)}, u32[]{:S(2)}) collective-permute-start(bf16[1,256,128]{2,1,0:T(8,128)(2,1)S(1)} %get-tuple-element.103), channel_id=1, source_target_pairs={{0,1},{1,2},{2,3},{3,4},{4,5},{5,6},{6,7},{7,8},{8,9},{9,10},{10,1... | collective-permute-start | bytes 196616 | tf_op jit(solution)/shard_map/while/body/eval_jaxpr/ppermute | solution.py:23
  178.2 17.3 %collective-permute-start = (bf16[1,4096,128]{2,1,0:T(8,128)(2,1)S(1)}, bf16[1,4096,128]{2,1,0:T(8,128)(2,1)S(1)}, u32[]{:S(2)}, u32[]{:S(2)}) collective-permute-start(bf16[1,4096,128]{2,1,0:T(8,128)(2,1)S(1)} %get-tuple-element.113), channel_id=1, source_target_pairs={{16,0},{32,16},{48,32},{64,48},{80,64},{96,80},{112,96},{128,112},... | collective-permute-start | bytes 3145736 | tf_op jit(solution)/shard_map/while/body/eval_jaxpr/ppermute | solution.py:13
  195.8 5.5 collective-permute-start.1
  197.7 7.1 %collective-permute-start.2 = (bf16[1,256,128]{2,1,0:T(8,128)(2,1)S(1)}, bf16[1,256,128]{2,1,0:T(8,128)(2,1)S(1)}, u32[]{:S(2)}, u32[]{:S(2)}) collective-permute-start(bf16[1,256,128]{2,1,0:T(8,128)(2,1)S(1)} %get-tuple-element.103), channel_id=1, source_target_pairs={{0,1},{1,2},{2,3},{3,4},{4,5},{5,6},{6,7},{7,8},{8,9},{9,10},{10,1... | collective-permute-start | bytes 196616 | tf_op jit(solution)/shard_map/while/body/eval_jaxpr/ppermute | solution.py:23
  212.7 17.3 %collective-permute-start = (bf16[1,4096,128]{2,1,0:T(8,128)(2,1)S(1)}, bf16[1,4096,128]{2,1,0:T(8,128)(2,1)S(1)}, u32[]{:S(2)}, u32[]{:S(2)}) collective-permute-start(bf16[1,4096,128]{2,1,0:T(8,128)(2,1)S(1)} %get-tuple-element.113), channel_id=1, source_target_pairs={{16,0},{32,16},{48,32},{64,48},{80,64},{96,80},{112,96},{128,112},... | collective-permute-start | bytes 3145736 | tf_op jit(solution)/shard_map/while/body/eval_jaxpr/ppermute | solution.py:13
  230.2 5.5 collective-permute-start.1
  232.2 7.1 %collective-permute-start.2 = (bf16[1,256,128]{2,1,0:T(8,128)(2,1)S(1)}, bf16[1,256,128]{2,1,0:T(8,128)(2,1)S(1)}, u32[]{:S(2)}, u32[]{:S(2)}) collective-permute-start(bf16[1,256,128]{2,1,0:T(8,128)(2,1)S(1)} %get-tuple-element.103), channel_id=1, source_target_pairs={{0,1},{1,2},{2,3},{3,4},{4,5},{5,6},{6,7},{7,8},{8,9},{9,10},{10,1... | collective-permute-start | bytes 196616 | tf_op jit(solution)/shard_map/while/body/eval_jaxpr/ppermute | solution.py:23
  247.2 17.3 %collective-permute-start = (bf16[1,4096,128]{2,1,0:T(8,128)(2,1)S(1)}, bf16[1,4096,128]{2,1,0:T(8,128)(2,1)S(1)}, u32[]{:S(2)}, u32[]{:S(2)}) collective-permute-start(bf16[1,4096,128]{2,1,0:T(8,128)(2,1)S(1)} %get-tuple-element.113), channel_id=1, source_target_pairs={{16,0},{32,16},{48,32},{64,48},{80,64},{96,80},{112,96},{128,112},... | collective-permute-start | bytes 3145736 | tf_op jit(solution)/shard_map/while/body/eval_jaxpr/ppermute | solution.py:13
  264.7 5.5 collective-permute-start.1
  266.6 7.1 %collective-permute-start.2 = (bf16[1,256,128]{2,1,0:T(8,128)(2,1)S(1)}, bf16[1,256,128]{2,1,0:T(8,128)(2,1)S(1)}, u32[]{:S(2)}, u32[]{:S(2)}) collective-permute-start(bf16[1,256,128]{2,1,0:T(8,128)(2,1)S(1)} %get-tuple-element.103), channel_id=1, source_target_pairs={{0,1},{1,2},{2,3},{3,4},{4,5},{5,6},{6,7},{7,8},{8,9},{9,10},{10,1... | collective-permute-start | bytes 196616 | tf_op jit(solution)/shard_map/while/body/eval_jaxpr/ppermute | solution.py:23
  281.7 17.3 %collective-permute-start = (bf16[1,4096,128]{2,1,0:T(8,128)(2,1)S(1)}, bf16[1,4096,128]{2,1,0:T(8,128)(2,1)S(1)}, u32[]{:S(2)}, u32[]{:S(2)}) collective-permute-start(bf16[1,4096,128]{2,1,0:T(8,128)(2,1)S(1)} %get-tuple-element.113), channel_id=1, source_target_pairs={{16,0},{32,16},{48,32},{64,48},{80,64},{96,80},{112,96},{128,112},... | collective-permute-start | bytes 3145736 | tf_op jit(solution)/shard_map/while/body/eval_jaxpr/ppermute | solution.py:13
  299.2 5.5 collective-permute-start.1
  301.1 7.1 %collective-permute-start.2 = (bf16[1,256,128]{2,1,0:T(8,128)(2,1)S(1)}, bf16[1,256,128]{2,1,0:T(8,128)(2,1)S(1)}, u32[]{:S(2)}, u32[]{:S(2)}) collective-permute-start(bf16[1,256,128]{2,1,0:T(8,128)(2,1)S(1)} %get-tuple-element.103), channel_id=1, source_target_pairs={{0,1},{1,2},{2,3},{3,4},{4,5},{5,6},{6,7},{7,8},{8,9},{9,10},{10,1... | collective-permute-start | bytes 196616 | tf_op jit(solution)/shard_map/while/body/eval_jaxpr/ppermute | solution.py:23
  316.2 17.3 %collective-permute-start = (bf16[1,4096,128]{2,1,0:T(8,128)(2,1)S(1)}, bf16[1,4096,128]{2,1,0:T(8,128)(2,1)S(1)}, u32[]{:S(2)}, u32[]{:S(2)}) collective-permute-start(bf16[1,4096,128]{2,1,0:T(8,128)(2,1)S(1)} %get-tuple-element.113), channel_id=1, source_target_pairs={{16,0},{32,16},{48,32},{64,48},{80,64},{96,80},{112,96},{128,112},... | collective-permute-start | bytes 3145736 | tf_op jit(solution)/shard_map/while/body/eval_jaxpr/ppermute | solution.py:13
  333.7 5.5 collective-permute-start.1
  335.6 7.1 %collective-permute-start.2 = (bf16[1,256,128]{2,1,0:T(8,128)(2,1)S(1)}, bf16[1,256,128]{2,1,0:T(8,128)(2,1)S(1)}, u32[]{:S(2)}, u32[]{:S(2)}) collective-permute-start(bf16[1,256,128]{2,1,0:T(8,128)(2,1)S(1)} %get-tuple-element.103), channel_id=1, source_target_pairs={{0,1},{1,2},{2,3},{3,4},{4,5},{5,6},{6,7},{7,8},{8,9},{9,10},{10,1... | collective-permute-start | bytes 196616 | tf_op jit(solution)/shard_map/while/body/eval_jaxpr/ppermute | solution.py:23
  350.7 17.3 %collective-permute-start = (bf16[1,4096,128]{2,1,0:T(8,128)(2,1)S(1)}, bf16[1,4096,128]{2,1,0:T(8,128)(2,1)S(1)}, u32[]{:S(2)}, u32[]{:S(2)}) collective-permute-start(bf16[1,4096,128]{2,1,0:T(8,128)(2,1)S(1)} %get-tuple-element.113), channel_id=1, source_target_pairs={{16,0},{32,16},{48,32},{64,48},{80,64},{96,80},{112,96},{128,112},... | collective-permute-start | bytes 3145736 | tf_op jit(solution)/shard_map/while/body/eval_jaxpr/ppermute | solution.py:13
  368.2 5.5 collective-permute-start.1
  370.1 7.1 %collective-permute-start.2 = (bf16[1,256,128]{2,1,0:T(8,128)(2,1)S(1)}, bf16[1,256,128]{2,1,0:T(8,128)(2,1)S(1)}, u32[]{:S(2)}, u32[]{:S(2)}) collective-permute-start(bf16[1,256,128]{2,1,0:T(8,128)(2,1)S(1)} %get-tuple-element.103), channel_id=1, source_target_pairs={{0,1},{1,2},{2,3},{3,4},{4,5},{5,6},{6,7},{7,8},{8,9},{9,10},{10,1... | collective-permute-start | bytes 196616 | tf_op jit(solution)/shard_map/while/body/eval_jaxpr/ppermute | solution.py:23
  385.1 17.3 %collective-permute-start = (bf16[1,4096,128]{2,1,0:T(8,128)(2,1)S(1)}, bf16[1,4096,128]{2,1,0:T(8,128)(2,1)S(1)}, u32[]{:S(2)}, u32[]{:S(2)}) collective-permute-start(bf16[1,4096,128]{2,1,0:T(8,128)(2,1)S(1)} %get-tuple-element.113), channel_id=1, source_target_pairs={{16,0},{32,16},{48,32},{64,48},{80,64},{96,80},{112,96},{128,112},... | collective-permute-start | bytes 3145736 | tf_op jit(solution)/shard_map/while/body/eval_jaxpr/ppermute | solution.py:13
  402.7 5.5 collective-permute-start.1
  404.6 7.1 %collective-permute-start.2 = (bf16[1,256,128]{2,1,0:T(8,128)(2,1)S(1)}, bf16[1,256,128]{2,1,0:T(8,128)(2,1)S(1)}, u32[]{:S(2)}, u32[]{:S(2)}) collective-permute-start(bf16[1,256,128]{2,1,0:T(8,128)(2,1)S(1)} %get-tuple-element.103), channel_id=1, source_target_pairs={{0,1},{1,2},{2,3},{3,4},{4,5},{5,6},{6,7},{7,8},{8,9},{9,10},{10,1... | collective-permute-start | bytes 196616 | tf_op jit(solution)/shard_map/while/body/eval_jaxpr/ppermute | solution.py:23
  419.6 17.3 %collective-permute-start = (bf16[1,4096,128]{2,1,0:T(8,128)(2,1)S(1)}, bf16[1,4096,128]{2,1,0:T(8,128)(2,1)S(1)}, u32[]{:S(2)}, u32[]{:S(2)}) collective-permute-start(bf16[1,4096,128]{2,1,0:T(8,128)(2,1)S(1)} %get-tuple-element.113), channel_id=1, source_target_pairs={{16,0},{32,16},{48,32},{64,48},{80,64},{96,80},{112,96},{128,112},... | collective-permute-start | bytes 3145736 | tf_op jit(solution)/shard_map/while/body/eval_jaxpr/ppermute | solution.py:13
  437.1 5.5 collective-permute-start.1
  439.1 7.1 %collective-permute-start.2 = (bf16[1,256,128]{2,1,0:T(8,128)(2,1)S(1)}, bf16[1,256,128]{2,1,0:T(8,128)(2,1)S(1)}, u32[]{:S(2)}, u32[]{:S(2)}) collective-permute-start(bf16[1,256,128]{2,1,0:T(8,128)(2,1)S(1)} %get-tuple-element.103), channel_id=1, source_target_pairs={{0,1},{1,2},{2,3},{3,4},{4,5},{5,6},{6,7},{7,8},{8,9},{9,10},{10,1... | collective-permute-start | bytes 196616 | tf_op jit(solution)/shard_map/while/body/eval_jaxpr/ppermute | solution.py:23
  454.1 17.3 %collective-permute-start = (bf16[1,4096,128]{2,1,0:T(8,128)(2,1)S(1)}, bf16[1,4096,128]{2,1,0:T(8,128)(2,1)S(1)}, u32[]{:S(2)}, u32[]{:S(2)}) collective-permute-start(bf16[1,4096,128]{2,1,0:T(8,128)(2,1)S(1)} %get-tuple-element.113), channel_id=1, source_target_pairs={{16,0},{32,16},{48,32},{64,48},{80,64},{96,80},{112,96},{128,112},... | collective-permute-start | bytes 3145736 | tf_op jit(solution)/shard_map/while/body/eval_jaxpr/ppermute | solution.py:13
  471.6 5.5 collective-permute-start.1
  473.6 7.1 %collective-permute-start.2 = (bf16[1,256,128]{2,1,0:T(8,128)(2,1)S(1)}, bf16[1,256,128]{2,1,0:T(8,128)(2,1)S(1)}, u32[]{:S(2)}, u32[]{:S(2)}) collective-permute-start(bf16[1,256,128]{2,1,0:T(8,128)(2,1)S(1)} %get-tuple-element.103), channel_id=1, source_target_pairs={{0,1},{1,2},{2,3},{3,4},{4,5},{5,6},{6,7},{7,8},{8,9},{9,10},{10,1... | collective-permute-start | bytes 196616 | tf_op jit(solution)/shard_map/while/body/eval_jaxpr/ppermute | solution.py:23
  488.6 17.3 %collective-permute-start = (bf16[1,4096,128]{2,1,0:T(8,128)(2,1)S(1)}, bf16[1,4096,128]{2,1,0:T(8,128)(2,1)S(1)}, u32[]{:S(2)}, u32[]{:S(2)}) collective-permute-start(bf16[1,4096,128]{2,1,0:T(8,128)(2,1)S(1)} %get-tuple-element.113), channel_id=1, source_target_pairs={{16,0},{32,16},{48,32},{64,48},{80,64},{96,80},{112,96},{128,112},... | collective-permute-start | bytes 3145736 | tf_op jit(solution)/shard_map/while/body/eval_jaxpr/ppermute | solution.py:13
  506.1 5.5 collective-permute-start.1
  508.0 7.1 %collective-permute-start.2 = (bf16[1,256,128]{2,1,0:T(8,128)(2,1)S(1)}, bf16[1,256,128]{2,1,0:T(8,128)(2,1)S(1)}, u32[]{:S(2)}, u32[]{:S(2)}) collective-permute-start(bf16[1,256,128]{2,1,0:T(8,128)(2,1)S(1)} %get-tuple-element.103), channel_id=1, source_target_pairs={{0,1},{1,2},{2,3},{3,4},{4,5},{5,6},{6,7},{7,8},{8,9},{9,10},{10,1... | collective-permute-start | bytes 196616 | tf_op jit(solution)/shard_map/while/body/eval_jaxpr/ppermute | solution.py:23
  523.1 17.3 %collective-permute-start = (bf16[1,4096,128]{2,1,0:T(8,128)(2,1)S(1)}, bf16[1,4096,128]{2,1,0:T(8,128)(2,1)S(1)}, u32[]{:S(2)}, u32[]{:S(2)}) collective-permute-start(bf16[1,4096,128]{2,1,0:T(8,128)(2,1)S(1)} %get-tuple-element.113), channel_id=1, source_target_pairs={{16,0},{32,16},{48,32},{64,48},{80,64},{96,80},{112,96},{128,112},... | collective-permute-start | bytes 3145736 | tf_op jit(solution)/shard_map/while/body/eval_jaxpr/ppermute | solution.py:13
  540.6 5.5 collective-permute-start.1
  542.5 7.1 %collective-permute-start.2 = (bf16[1,256,128]{2,1,0:T(8,128)(2,1)S(1)}, bf16[1,256,128]{2,1,0:T(8,128)(2,1)S(1)}, u32[]{:S(2)}, u32[]{:S(2)}) collective-permute-start(bf16[1,256,128]{2,1,0:T(8,128)(2,1)S(1)} %get-tuple-element.103), channel_id=1, source_target_pairs={{0,1},{1,2},{2,3},{3,4},{4,5},{5,6},{6,7},{7,8},{8,9},{9,10},{10,1... | collective-permute-start | bytes 196616 | tf_op jit(solution)/shard_map/while/body/eval_jaxpr/ppermute | solution.py:23
  (2 other events, 5.1 us)
where the time goes:
time: 584 us; the launch traced here: 582 us
  waiting for transfers between devices  304 us (52%)
  starting transfers between devices  117 us (20%)
  matrix products  79.1 us (14%)
  local copies, waits for them, and re-layouts  75.1 us (13%)
    ppermute x16, waiting for transfers between devices, passed_along(): return lax.ppermute(value, axis, pairs)  246 us
    dot_general x16, matrix products, advance(): jnp.einsum('rtopq,rtpqk->rtok', blocks, picked, preferred_element_type=jn...  75.3 us
    ppermute x16, waiting for transfers between devices, padded(): before = lax.ppermute(last, axis, up)  57.9 us
    gather x64, local copies, waits for them, and re-layouts, one_row(): return row_blocks[row_sources]  52.9 us
    ppermute x16, starting transfers between devices, padded(): before = lax.ppermute(last, axis, up)  52.4 us
    ppermute x16, starting transfers between devices, padded(): after = lax.ppermute(leading, axis, down)  33.4 us
    ppermute x16, starting transfers between devices, passed_along(): return lax.ppermute(value, axis, pairs)  31.4 us
    unnamed x5, local copies, waits for them, and re-layouts  21.7 us
  transfers between devices with their start and end apart: 48, of which 32 were waited for; matrix products, arithmetic and copies ran while one was open for 1% of the time, Pallas kernels for 0%

commit v1 on v0

v1 whole, which is shorter than its diff:
```python
import functools

import jax
import jax.numpy as jnp
from jax import lax
from jax.experimental import pallas as pl
from jax.experimental.pallas import tpu as pltpu
from jax.sharding import PartitionSpec as P

TILE = 128
REACH = 2
CHUNK = REACH * TILE
MESH = pl.DeviceIdType.MESH


def sweep_kernel(
    ncol, nsec, src_ref, env_hbm, a_hbm, left_hbm, env_out, grad_out,
    a_v, left_v, land, win, fresh, grad_v,
    recv_sem, send_sem, a_sem, left_sem, out_sem, gout_sem,
):
    col = lax.axis_index("col")
    sec = lax.axis_index("sec")
    chunks = a_v.shape[0] // CHUNK
    tiles = a_v.shape[0] // TILE
    pairs = src_ref.shape[0]
    odd = sec % 2
    first = col == ncol - 1
    has_below = sec > 0
    has_above = sec < nsec - 1

    def place(m):
        return m + odd * (chunks - 1 - 2 * m)

    def slot(m):
        return place(m) + 1

    def rows(q):
        return pl.ds(pl.multiple_of(q * CHUNK, CHUNK), CHUNK)

    def exists(w):
        return jnp.logical_and(jnp.logical_or(w > 0, has_below), jnp.logical_or(w <= chunks, has_above))

    def arrival(w):
        return pltpu.make_async_copy(land.at[rows(w)], land.at[rows(w)], recv_sem.at[w])

    def load_a(q):
        return pltpu.make_async_copy(a_hbm.at[rows(q)], a_v.at[rows(q)], a_sem.at[q])

    def load_left(q):
        return pltpu.make_async_copy(left_hbm.at[rows(q)], left_v.at[rows(q)], left_sem.at[q])

    def load_env(q):
        return pltpu.make_async_copy(env_hbm.at[rows(q)], land.at[rows(q + 1)], recv_sem.at[q + 1])

    def store_env(q):
        return pltpu.make_async_copy(fresh.at[rows(q)], env_out.at[rows(q)], out_sem.at[q])

    def store_grad(q):
        return pltpu.make_async_copy(grad_v.at[rows(q)], grad_out.at[rows(q)], gout_sem.at[q])

    def send(src, q, w, sem, to_col, to_sec):
        return pltpu.make_async_remote_copy(
            src_ref=src.at[rows(q)],
            dst_ref=land.at[rows(w)],
            send_sem=send_sem.at[sem],
            recv_sem=recv_sem.at[w],
            device_id=(to_col, to_sec),
            device_id_type=MESH,
        )

    barrier = pltpu.get_barrier_semaphore()

    def greet(to_col, to_sec):
        pl.semaphore_signal(barrier, inc=1, device_id=(to_col, to_sec), device_id_type=MESH)

    @pl.when(jnp.logical_not(first))
    def _():
        greet(col + 1, sec)

        @pl.when(has_below)
        def _():
            greet(col + 1, sec - 1)

        @pl.when(has_above)
        def _():
            greet(col + 1, sec + 1)

    @pl.when(first)
    def _():
        @pl.when(has_below)
        def _():
            greet(col, sec - 1)

        @pl.when(has_above)
        def _():
            greet(col, sec + 1)

    def start_loads(m, carry):
        q = place(m)

        @pl.when(first)
        def _():
            load_env(q).start()

        load_a(q).start()
        load_left(q).start()
        return carry

    lax.fori_loop(0, chunks, start_loads, 0)
    win[...] = jnp.zeros_like(win)

    def count(flag):
        return flag.astype(jnp.int32)

    beside = count(has_below) + count(has_above)

    @pl.when(col > 0)
    def _():
        pl.semaphore_wait(barrier, 1 + beside + count(first) * beside)

    @pl.when(first)
    def _():
        @pl.when(has_below)
        def _():
            send(env_hbm, 0, chunks + 1, chunks + 2, col, sec - 1).start()

        @pl.when(has_above)
        def _():
            send(env_hbm, chunks - 1, 0, chunks + 3, col, sec + 1).start()

    def take(w):
        @pl.when(exists(w))
        def _():
            arrival(w).wait()
            for u in range(REACH):
                win[w * REACH + u] = land[pl.ds(pl.multiple_of(w * CHUNK, CHUNK) + u * TILE, TILE), :]

    take(slot(-1))
    take(slot(0))

    def step(m, carry):
        q = place(m)
        take(slot(m + 1))
        load_a(q).wait()

        def picked(t):
            parts = []
            for j in range(pairs):
                i = src_ref[j, t] - sec * tiles + REACH
                parts.append(win[jnp.clip(i, 0, win.shape[0] - 1)])
            return jnp.concatenate(parts, axis=0)

        def tile_rows(t):
            return pl.ds(pl.multiple_of(t * TILE, TILE), TILE)

        for u in range(REACH):
            t = q * REACH + u
            acc = jnp.dot(a_v[tile_rows(t), :], picked(t), preferred_element_type=jnp.float32)
            fresh[tile_rows(t), :] = acc.astype(jnp.bfloat16)

        @pl.when(col > 0)
        def _():
            send(fresh, q, q + 1, q, col - 1, sec).start()

            @pl.when(jnp.logical_and(q == 0, has_below))
            def _():
                send(fresh, 0, chunks + 1, chunks, col - 1, sec - 1).start()

            @pl.when(jnp.logical_and(q == chunks - 1, has_above))
            def _():
                send(fresh, chunks - 1, 0, chunks + 1, col - 1, sec + 1).start()

        store_env(q).start()
        load_left(q).wait()
        for u in range(REACH):
            t = q * REACH + u
            g = lax.dot_general(
                left_v[tile_rows(t), :], picked(t), (((1,), (1,)), ((), ())), preferred_element_type=jnp.float32
            )
            grad_v[tile_rows(t), :] = g.astype(jnp.bfloat16)
        store_grad(q).start()
        return carry

    lax.fori_loop(0, chunks, step, 0)

    def drain(q, carry):
        store_env(q).wait()
        store_grad(q).wait()

        @pl.when(col > 0)
        def _():
            send(fresh, q, q + 1, q, col - 1, sec).wait_send()

        return carry

    lax.fori_loop(0, chunks, drain, 0)

    @pl.when(jnp.logical_and(col > 0, has_below))
    def _():
        send(fresh, 0, chunks + 1, chunks, col - 1, sec - 1).wait_send()

    @pl.when(jnp.logical_and(col > 0, has_above))
    def _():
        send(fresh, chunks - 1, 0, chunks + 1, col - 1, sec + 1).wait_send()

    @pl.when(jnp.logical_and(first, has_below))
    def _():
        send(env_hbm, 0, chunks + 1, chunks + 2, col, sec - 1).wait_send()

    @pl.when(jnp.logical_and(first, has_above))
    def _():
        send(env_hbm, chunks - 1, 0, chunks + 3, col, sec + 1).wait_send()


def per_device(env_right, transfer, sources, env_left):
    ncol = lax.axis_size("col")
    nsec = lax.axis_size("sec")
    length = transfer.shape[2]
    pairs = transfer.shape[3]
    width = env_right.shape[2]
    chunks = length // CHUNK
    a = transfer.reshape(length, pairs * TILE)
    left = env_left.reshape(length, width)
    src = jnp.transpose(sources.reshape(length // TILE, pairs))
    bf16 = jnp.bfloat16
    anywhere = pl.BlockSpec(memory_space=pl.ANY)
    env, grad = pl.pallas_call(
        functools.partial(sweep_kernel, ncol, nsec),
        out_shape=(
            jax.ShapeDtypeStruct((length, width), bf16),
            jax.ShapeDtypeStruct((length, pairs * TILE), bf16),
        ),
        in_specs=[pl.BlockSpec(memory_space=pltpu.SMEM), anywhere, anywhere, anywhere],
        out_specs=(anywhere, anywhere),
        scratch_shapes=[
            pltpu.VMEM((length, pairs * TILE), bf16),
            pltpu.VMEM((length, width), bf16),
            pltpu.VMEM((length + 2 * CHUNK, width), bf16),
            pltpu.VMEM((length // TILE + 2 * REACH, TILE, width), bf16),
            pltpu.VMEM((length, width), bf16),
            pltpu.VMEM((length, pairs * TILE), bf16),
            pltpu.SemaphoreType.DMA((chunks + 2,)),
            pltpu.SemaphoreType.DMA((chunks + 4,)),
            pltpu.SemaphoreType.DMA((chunks,)),
            pltpu.SemaphoreType.DMA((chunks,)),
            pltpu.SemaphoreType.DMA((chunks,)),
            pltpu.SemaphoreType.DMA((chunks,)),
        ],
        compiler_params=pltpu.CompilerParams(
            collective_id=0, has_side_effects=True, vmem_limit_bytes=24 * 1024 * 1024
        ),
        name="sweep",
    )(src, env_right.reshape(length, width), a, left)
    return env.reshape(1, 1, length, width), grad.reshape(1, 1, length, pairs, TILE)


def solution(mesh):
    placed = (
        P(None, "sec", None),
        P("col", None, "sec", None, None),
        P("col", None, "sec", None),
        P("col", None, "sec", None),
    )
    return jax.shard_map(
        per_device,
        mesh=mesh,
        in_specs=placed,
        out_specs=(P("col", None, "sec", None), P("col", None, "sec", None, None)),
        check_vma=False,
    )
```

time: 584 us -> 107 us (0.18)
  the two profiles are of different devices: /device:TPU:121 before, /device:TPU:24 now
where the time goes in v1:
time: 107 us; the launch traced here: 106 us
  Pallas kernels  92.9 us (87%)
  local copies, waits for them, and re-layouts  12.9 us (12%)
    pallas_call x1, Pallas kernels, per_device(): pl.pallas_call(functools.partial(sweep_kernel, ncol, nsec), out_shape=(ja...  92.9 us
    reshape x1, local copies, waits for them, and re-layouts, per_device(): grad.reshape(1, 1, length, pairs, TILE)  6.88 us
    unnamed x10, local copies, waits for them, and re-layouts  5.97 us

profile of v1, /device:TPU:24, one launch (start us, length us, event | category | flops | bytes accessed | tf_op | source)
XLA Modules:
  0.0 106.4 jit_solution(3398417780427448734)
XLA Ops:
  0.6 0.0 copy-start.1
  0.6 0.0 copy-start.2
  0.7 0.0 copy-start.3
  0.7 3.1 %copy.8 = bf16[512,8,4,128]{3,1,2,0:T(8,128)(2,1)S(1)} copy(bf16[512,8,4,128]{3,2,1,0:T(4,128)(2,1)} %bitcast.16) | data formatting | bytes 8388608
  3.7 0.0 copy-done.1
  3.7 0.0 copy-done.2
  3.7 0.0 copy-done.3
  3.7 92.9 %sweep.1 = (bf16[4096,128]{1,0:T(8,128)(2,1)S(1)}, bf16[4096,512]{1,0:T(8,128)(2,1)S(1)}) custom-call(s32[4,32]{1,0:T(4,128)S(1)} %bitcast.15, bf16[4096,128]{1,0:T(8,128)(2,1)S(1)} %bitcast.13, bf16[4096,512]{1,0:T(8,128)(2,1)S(1)} %bitcast.11, bf16[4096,128]{1,0:T(8,128)(2,1)S(1)} %bitcast.14), custom_call_target="tpu_custom_call" | custom-call | tf_op jit(solution)/shard_map/sweep/pallas_call | solution.py:227
  96.6 0.0 copy-start
  96.6 1.9 %copy-done = bf16[4096,512]{1,0:T(8,128)(2,1)} copy-done((bf16[4096,512]{1,0:T(8,128)(2,1)}, bf16[4096,512]{1,0:T(8,128)(2,1)S(1)}, u32[]{:S(2)}) %copy-start) | copy-done | bytes 4194328
  98.6 6.9 %reshape.27 = bf16[1,1,4096,4,128]{4,3,2,1,0:T(4,128)(2,1)} reshape(bf16[4096,512]{1,0:T(8,128)(2,1)} %copy-done) | data formatting | bytes 8388608 | tf_op jit(solution)/shard_map/reshape | solution.py:254
  105.5 1.0 copy.10
Async XLA Ops:
  0.6 3.1 %copy-start.1 = (bf16[1,4096,128]{2,1,0:T(8,128)(2,1)S(1)}, bf16[1,4096,128]{2,1,0:T(8,128)(2,1)}, u32[]{:S(2)}) copy-start(bf16[1,4096,128]{2,1,0:T(8,128)(2,1)} %param.4) | copy-start | bytes 3145732
  0.6 3.1 %copy-start.2 = (bf16[1,1,4096,128]{3,2,1,0:T(8,128)(2,1)S(1)}, bf16[1,1,4096,128]{3,2,1,0:T(8,128)(2,1)}, u32[]{:S(2)}) copy-start(bf16[1,1,4096,128]{3,2,1,0:T(8,128)(2,1)} %param.7) | copy-start | bytes 3145732
  0.7 3.1 %copy-start.3 = (s32[1,1,32,4]{2,3,1,0:T(4,128)S(1)}, s32[1,1,32,4]{2,3,1,0:T(4,128)}, u32[]{:S(2)}) copy-start(s32[1,1,32,4]{2,3,1,0:T(4,128)} %param.6) | copy-start | bytes 1540
  96.6 1.9 %copy-start = (bf16[4096,512]{1,0:T(8,128)(2,1)}, bf16[4096,512]{1,0:T(8,128)(2,1)S(1)}, u32[]{:S(2)}) copy-start(bf16[4096,512]{1,0:T(8,128)(2,1)S(1)} %get-tuple-element.5) | copy-start | bytes 12582916

commit v2 on v0

v2 whole, which is shorter than its diff:
```python
import functools

import jax
import jax.numpy as jnp
from jax import lax
from jax.experimental import pallas as pl
from jax.experimental.pallas import tpu as pltpu
from jax.sharding import PartitionSpec as P

TILE = 128
REACH = 2
INLINE_GRAD = 2
MESH = pl.DeviceIdType.MESH


def sweep_kernel(
    ncol, nsec, pairs, src_ref, env_hbm, b_hbm, left_hbm, env_out, grad_out,
    b_v, a_v, left_v, land, win, fresh, grad_v, wide,
    recv_sem, send_sem, b_sem, left_sem, out_sem, gout_sem,
):
    col = lax.axis_index("col")
    sec = lax.axis_index("sec")
    tiles = left_v.shape[0] // TILE
    odd = sec % 2
    first = col == ncol - 1
    has_below = sec > 0
    has_above = sec < nsec - 1
    side = 2 * odd - 1
    has_pre = jnp.logical_and(sec + side >= 0, sec + side < nsec)
    has_post = jnp.logical_and(sec - side >= 0, sec - side < nsec)

    def local(p):
        return p + odd * (tiles - 1 - 2 * p)

    def slot(p):
        return local(p) + REACH

    def slot_beside(p):
        return tiles - 1 - p + odd * (2 * p + 1 - tiles) + REACH

    def rows(t):
        return pl.ds(pl.multiple_of(t * TILE, TILE), TILE)

    def mixed(t):
        return pl.ds(pl.multiple_of(t * pairs * TILE, pairs * TILE), pairs * TILE)

    def load_b(t):
        return pltpu.make_async_copy(b_hbm.at[mixed(t)], b_v.at[mixed(t)], b_sem.at[t])

    def load_left():
        return pltpu.make_async_copy(left_hbm, left_v, left_sem)

    def load_env(t):
        return pltpu.make_async_copy(env_hbm.at[rows(t)], land.at[t + REACH], recv_sem.at[t + REACH])

    def store_env(t):
        return pltpu.make_async_copy(fresh.at[rows(t)], env_out.at[rows(t)], out_sem.at[t])

    def store_grad(t):
        return pltpu.make_async_copy(grad_v.at[mixed(t)], grad_out.at[mixed(t)], gout_sem.at[t])

    def send(src, t, w, sem, to_col, to_sec):
        return pltpu.make_async_remote_copy(
            src_ref=src.at[rows(t)],
            dst_ref=land.at[w],
            send_sem=send_sem.at[sem],
            recv_sem=recv_sem.at[w],
            device_id=(to_col, to_sec),
            device_id_type=MESH,
        )

    def send_on(p):
        return send(fresh, local(p), slot(p), p, col - 1, sec)

    def send_pre(src, p, to_col, at):
        return send(src, local(p), slot_beside(-1 - p), tiles + at + p, to_col, sec + side)

    def send_post(src, p, to_col, at):
        return send(src, local(p), slot_beside(2 * tiles - 1 - p), tiles + at + p - tiles + 2 * REACH, to_col, sec - side)

    barrier = pltpu.get_barrier_semaphore()

    def greet(to_col, to_sec):
        pl.semaphore_signal(barrier, inc=1, device_id=(to_col, to_sec), device_id_type=MESH)

    @pl.when(jnp.logical_not(first))
    def _():
        greet(col + 1, sec)

    behind = jnp.minimum(col + 1, ncol - 1)

    @pl.when(has_below)
    def _():
        greet(behind, sec - 1)

    @pl.when(has_above)
    def _():
        greet(behind, sec + 1)

    def start_loads(p, carry):
        t = local(p)

        @pl.when(first)
        def _():
            load_env(t).start()

        load_b(t).start()
        return carry

    lax.fori_loop(0, tiles, start_loads, 0)
    load_left().start()

    def count(flag):
        return flag.astype(jnp.int32)

    beside = count(has_below) + count(has_above)

    @pl.when(col > 0)
    def _():
        pl.semaphore_wait(barrier, 1 + beside + count(first) * beside)

    def edges(do):
        @pl.when(jnp.logical_and(first, has_pre))
        def _():
            for u in range(REACH):
                do(send_pre(env_hbm, u, col, 2 * REACH))

        @pl.when(jnp.logical_and(first, has_post))
        def _():
            for u in range(REACH):
                do(send_post(env_hbm, tiles - REACH + u, col, 2 * REACH))

    edges(lambda copy: copy.start())
    win[...] = jnp.zeros_like(win)

    def sort_rows(t):
        load_b(t).wait()
        wide[...] = b_v[mixed(t), :].astype(jnp.float32)
        for j in range(pairs):
            part = wide[pl.ds(j, TILE, stride=pairs), :]
            a_v[rows(t), j * TILE:(j + 1) * TILE] = part.astype(jnp.bfloat16)

    @pl.when(jnp.logical_not(first))
    def _():
        def one(p, carry):
            sort_rows(local(p))
            return carry

        lax.fori_loop(0, tiles, one, 0)

    def take(p):
        w = slot(p)
        pltpu.make_async_copy(land.at[w], land.at[w], recv_sem.at[w]).wait()
        win[w] = land[w]

    @pl.when(has_pre)
    def _():
        for u in range(REACH):
            take(-1 - u)

    for u in range(REACH):
        take(u)

    def picked(t):
        parts = []
        for j in range(pairs):
            i = src_ref[j, t] - sec * tiles + REACH
            parts.append(win[jnp.clip(i, 0, win.shape[0] - 1)])
        return jnp.concatenate(parts, axis=0)

    def gradient(t):
        g = lax.dot_general(
            left_v[rows(t), :], picked(t), (((1,), (1,)), ((), ())), preferred_element_type=jnp.float32
        )
        for j in range(pairs):
            wide[pl.ds(j, TILE, stride=pairs), :] = g[:, j * TILE:(j + 1) * TILE]
        grad_v[mixed(t), :] = wide[...].astype(jnp.bfloat16)
        store_grad(t).start()

    load_left().wait()

    def step(p, carry):
        t = local(p)

        @pl.when(first)
        def _():
            sort_rows(t)

        @pl.when(jnp.logical_or(p + REACH < tiles, has_post))
        def _():
            take(p + REACH)

        acc = jnp.dot(a_v[rows(t), :], picked(t), preferred_element_type=jnp.float32)
        fresh[rows(t), :] = acc.astype(jnp.bfloat16)

        @pl.when(col > 0)
        def _():
            @pl.when(jnp.logical_and(p < REACH, has_pre))
            def _():
                send_pre(fresh, p, col - 1, 0).start()

            send_on(p).start()

            @pl.when(jnp.logical_and(p >= tiles - REACH, has_post))
            def _():
                send_post(fresh, p, col - 1, 0).start()

        store_env(t).start()

        @pl.when(col < INLINE_GRAD)
        def _():
            gradient(t)

        return carry

    lax.fori_loop(0, tiles, step, 0)

    @pl.when(col >= INLINE_GRAD)
    def _():
        def one(p, carry):
            gradient(local(p))
            return carry

        lax.fori_loop(0, tiles, one, 0)

    def drain(p, carry):
        store_env(local(p)).wait()
        store_grad(local(p)).wait()

        @pl.when(col > 0)
        def _():
            send_on(p).wait_send()

        return carry

    lax.fori_loop(0, tiles, drain, 0)

    @pl.when(jnp.logical_and(col > 0, has_pre))
    def _():
        for u in range(REACH):
            send_pre(fresh, u, col - 1, 0).wait_send()

    @pl.when(jnp.logical_and(col > 0, has_post))
    def _():
        for u in range(REACH):
            send_post(fresh, tiles - REACH + u, col - 1, 0).wait_send()

    edges(lambda copy: copy.wait_send())


def per_device(env_right, transfer, sources, env_left):
    ncol = lax.axis_size("col")
    nsec = lax.axis_size("sec")
    length = transfer.shape[2]
    pairs = transfer.shape[3]
    width = env_right.shape[2]
    tiles = length // TILE
    b = transfer.reshape(length * pairs, TILE)
    left = env_left.reshape(length, width)
    src = jnp.transpose(sources.reshape(tiles, pairs))
    bf16 = jnp.bfloat16
    in_hbm = pl.BlockSpec(memory_space=pltpu.HBM)
    anywhere = pl.BlockSpec(memory_space=pl.ANY)
    env, grad = pl.pallas_call(
        functools.partial(sweep_kernel, ncol, nsec, pairs),
        out_shape=(
            jax.ShapeDtypeStruct((length, width), bf16),
            jax.ShapeDtypeStruct((length * pairs, TILE), bf16),
        ),
        in_specs=[pl.BlockSpec(memory_space=pltpu.SMEM), in_hbm, in_hbm, in_hbm],
        out_specs=(anywhere, anywhere),
        scratch_shapes=[
            pltpu.VMEM((length * pairs, TILE), bf16),
            pltpu.VMEM((length, pairs * TILE), bf16),
            pltpu.VMEM((length, width), bf16),
            pltpu.VMEM((tiles + 2 * REACH, TILE, width), bf16),
            pltpu.VMEM((tiles + 2 * REACH, TILE, width), bf16),
            pltpu.VMEM((length, width), bf16),
            pltpu.VMEM((length * pairs, TILE), bf16),
            pltpu.VMEM((pairs * TILE, TILE), jnp.float32),
            pltpu.SemaphoreType.DMA((tiles + 2 * REACH,)),
            pltpu.SemaphoreType.DMA((tiles + 4 * REACH,)),
            pltpu.SemaphoreType.DMA((tiles,)),
            pltpu.SemaphoreType.DMA,
            pltpu.SemaphoreType.DMA((tiles,)),
            pltpu.SemaphoreType.DMA((tiles,)),
        ],
        compiler_params=pltpu.CompilerParams(
            collective_id=0, has_side_effects=True, vmem_limit_bytes=24 * 1024 * 1024
        ),
        name="sweep",
    )(src, *(pltpu.with_memory_space_constraint(x, pltpu.HBM) for x in (env_right.reshape(length, width), b, left)))
    return env.reshape(1, 1, length, width), grad.reshape(1, 1, length, pairs, TILE)


def solution(mesh):
    placed = (
        P(None, "sec", None),
        P("col", None, "sec", None, None),
        P("col", None, "sec", None),
        P("col", None, "sec", None),
    )
    return jax.shard_map(
        per_device,
        mesh=mesh,
        in_specs=placed,
        out_specs=(P("col", None, "sec", None), P("col", None, "sec", None, None)),
        check_vma=False,
    )
```

time: 584 us -> 106 us (0.18)
  the two profiles are of different devices: /device:TPU:121 before, /device:TPU:24 now
where the time goes in v2:
time: 106 us
  Pallas kernels  102 us (96%)
  local copies, waits for them, and re-layouts  3.66 us (3%)
    pallas_call x1, Pallas kernels, per_device(): pl.pallas_call(functools.partial(sweep_kernel, ncol, nsec, pairs), out_sh...  102 us
    unnamed x4, local copies, waits for them, and re-layouts  3.66 us

profile of v2, /device:TPU:24, one launch (start us, length us, event | category | flops | bytes accessed | tf_op | source)
XLA Modules:
  0.0 105.9 jit_solution(5973469824488611295)
XLA Ops:
  0.6 0.0 copy-start
  0.6 0.7 copy-done
  1.3 101.6 %sweep.1 = (bf16[4096,128]{1,0:T(8,128)(2,1)S(1)}, bf16[16384,128]{1,0:T(8,128)(2,1)S(1)}) custom-call(s32[4,32]{1,0:T(4,128)S(1)} %bitcast.10, bf16[4096,128]{1,0:T(8,128)(2,1)} %bitcast.12, bf16[16384,128]{1,0:T(8,128)(2,1)} %bitcast.11, bf16[4096,128]{1,0:T(8,128)(2,1)} %bitcast.13), custom_call_target="tpu_custom_call" | custom-call | tf_op jit(solution)/shard_map/sweep/pallas_call | solution.py:264
  102.9 1.0 copy.8
  103.8 2.0 %copy.9 = bf16[1,1,4096,4,128]{4,3,2,1,0:T(4,128)(2,1)} copy(bf16[1,1,4096,4,128]{4,3,2,1,0:T(4,128)(2,1)S(1)} %bitcast.8) | data formatting | bytes 8388608
Async XLA Ops:
  0.6 0.7 copy-start

commit v3 on v2

v3 whole, which is shorter than its diff:
```python
import functools

import jax
import jax.numpy as jnp
from jax import lax
from jax.experimental import pallas as pl
from jax.experimental.pallas import tpu as pltpu
from jax.sharding import PartitionSpec as P

TILE = 128
REACH = 2
EDGE = 2 * REACH
GROUP = 4
MESH = pl.DeviceIdType.MESH


def sweep_kernel(
    ncol, nsec, pairs, src_ref, env_hbm, b_hbm, left_hbm, env_out, grad_out,
    b_v, a_v, left_v, env_v, land, win, fresh, grad_v, wide, spread, halo_a,
    recv_sem, send_sem, b_sem, left_sem, env_sem, out_sem, gout_sem, spread_sem, halo_sem,
):
    col = lax.axis_index("col")
    sec = lax.axis_index("sec")
    tiles = left_v.shape[0] // TILE
    groups = tiles // GROUP
    odd = sec % 2
    first = col == ncol - 1
    wider = jnp.logical_and(col % 2 == 1, jnp.logical_not(first))
    has_below = sec > 0
    has_above = sec < nsec - 1
    side = 2 * odd - 1
    has_pre = jnp.logical_and(sec + side >= 0, sec + side < nsec)
    has_post = jnp.logical_and(sec - side >= 0, sec - side < nsec)

    def local(p):
        return p + odd * (tiles - 1 - 2 * p)

    def slot(p):
        return local(p) + EDGE

    def slot_beside(p):
        return tiles - 1 - p + odd * (2 * p + 1 - tiles) + EDGE

    def rows(t):
        return pl.ds(pl.multiple_of(t * TILE, TILE), TILE)

    def mixed(t, n=1):
        return pl.ds(pl.multiple_of(t * pairs * TILE, pairs * TILE), n * pairs * TILE)

    def load_b(g):
        span = mixed(g * GROUP, GROUP)
        return pltpu.make_async_copy(b_hbm.at[span], b_v.at[span], b_sem.at[g])

    load_left = pltpu.make_async_copy(left_hbm, left_v, left_sem)
    load_env = pltpu.make_async_copy(env_hbm, env_v, env_sem)
    store_env = pltpu.make_async_copy(fresh.at[pl.ds(REACH, tiles)], env_out, out_sem)

    def store_grad(i):
        span = mixed(2 * i, 2)
        return pltpu.make_async_copy(grad_v.at[span], grad_out.at[span], gout_sem.at[i])

    def send(src, w, sem, to_col, to_sec):
        return pltpu.make_async_remote_copy(
            src_ref=src,
            dst_ref=land.at[w],
            send_sem=send_sem.at[sem],
            recv_sem=recv_sem.at[w],
            device_id=(to_col, to_sec),
            device_id_type=MESH,
        )

    def held(p):
        return fresh.at[local(p) + REACH]

    def send_on(p):
        return send(held(p), slot(p), p + REACH, col - 1, sec)

    after = tiles + 2 * REACH

    def send_pre(src, p, to_col, at):
        return send(src, slot_beside(-1 - p), after + at + p, to_col, sec + side)

    def send_post(src, p, to_col, at):
        return send(src, slot_beside(2 * tiles - 1 - p), after + at + EDGE + tiles - 1 - p, to_col, sec - side)

    def send_spread(h, to_sec):
        return pltpu.make_async_remote_copy(
            src_ref=spread.at[h],
            dst_ref=halo_a.at[h],
            send_sem=spread_sem.at[h],
            recv_sem=halo_sem.at[h],
            device_id=(col, to_sec),
            device_id_type=MESH,
        )

    barrier = pltpu.get_barrier_semaphore()

    def greet(to_col, to_sec):
        pl.semaphore_signal(barrier, inc=1, device_id=(to_col, to_sec), device_id_type=MESH)

    @pl.when(jnp.logical_not(first))
    def _():
        greet(col + 1, sec)

    behind = jnp.minimum(col + 1, ncol - 1)
    meets = jnp.logical_or(col % 2 == 1, col == ncol - 2)
    for there, by in ((has_below, -1), (has_above, 1)):
        @pl.when(jnp.logical_and(there, meets))
        def _():
            greet(behind, sec + by)

        @pl.when(jnp.logical_and(there, wider))
        def _():
            greet(col, sec + by)

    @pl.when(first)
    def _():
        load_env.start()

    def start_loads(i, carry):
        load_b(i + odd * (groups - 1 - 2 * i)).start()
        return carry

    lax.fori_loop(0, groups, start_loads, 0)
    load_left.start()

    def count(flag):
        return flag.astype(jnp.int32)

    beside = count(has_below) + count(has_above)

    @pl.when(col > 0)
    def _():
        pl.semaphore_wait(barrier, 1 + beside + count(first) * beside)

    def first_edges(do):
        @pl.when(jnp.logical_and(first, has_pre))
        def _():
            for u in range(REACH):
                do(send_pre(env_hbm.at[rows(local(u))], u, col, 2 * EDGE))

        @pl.when(jnp.logical_and(first, has_post))
        def _():
            for u in range(REACH):
                p = tiles - 1 - u
                do(send_post(env_hbm.at[rows(local(p))], p, col, 2 * EDGE))

    first_edges(lambda copy: copy.start())
    win[...] = jnp.zeros_like(win)

    def sort_rows(t):
        wide[0] = b_v[mixed(t), :].astype(jnp.float32)
        for j in range(pairs):
            part = wide[0, pl.ds(j, TILE, stride=pairs), :]
            a_v[rows(t), j * TILE:(j + 1) * TILE] = part.astype(jnp.bfloat16)

    def sort_group(i):
        g = i + odd * (groups - 1 - 2 * i)
        load_b(g).wait()
        for u in range(GROUP):
            sort_rows(g * GROUP + u)

    def by_offset(t, h):
        blocks = [a_v[rows(t), j * TILE:(j + 1) * TILE].astype(jnp.float32) for j in range(pairs)]
        for k in range(2 * REACH + 1):
            total = jnp.zeros((TILE, TILE), jnp.float32)
            for j in range(pairs):
                here = src_ref[j, t] - sec * tiles - t == k - REACH
                total = total + jnp.where(here, blocks[j], 0.0)
            spread[h, :, k * TILE:(k + 1) * TILE] = total.astype(jnp.bfloat16)

    def edge_spreads(do):
        @pl.when(jnp.logical_and(wider, has_pre))
        def _():
            for u in range(REACH):
                do(u, send_spread(u, sec + side))

        @pl.when(jnp.logical_and(wider, has_post))
        def _():
            for u in range(REACH):
                do(tiles - 1 - u, send_spread(REACH + u, sec - side))

    @pl.when(jnp.logical_not(first))
    def _():
        sort_group(0)
        sort_group(groups - 1)

        @pl.when(wider)
        def _():
            for u in range(REACH):
                by_offset(local(u), u)
                by_offset(local(tiles - 1 - u), REACH + u)

        edge_spreads(lambda p, copy: copy.start())

        def one(i, carry):
            sort_group(i)
            return carry

        lax.fori_loop(1, groups - 1, one, 0)

    load_left.wait()

    def arrive(p):
        w = slot(p)
        pltpu.make_async_copy(land.at[w], land.at[w], recv_sem.at[w]).wait()
        win[w] = land[w]

    def take(p):
        @pl.when(first)
        def _():
            win[slot(p)] = env_v[rows(local(p)), :]

        @pl.when(jnp.logical_not(first))
        def _():
            arrive(p)

    @pl.when(first)
    def _():
        load_env.wait()

    def picked(t):
        parts = []
        for j in range(pairs):
            i = src_ref[j, t] - sec * tiles + EDGE
            parts.append(win[jnp.clip(i, 0, win.shape[0] - 1)])
        return jnp.concatenate(parts, axis=0)

    def halo_tiles(ps, hs):
        for p, h in zip(ps, hs):
            w = slot(p)
            near = win[pl.ds(w - REACH, 2 * REACH + 1)].reshape((2 * REACH + 1) * TILE, TILE)
            acc = jnp.dot(halo_a[h], near, preferred_element_type=jnp.float32)
            fresh[local(p) + REACH] = acc.astype(jnp.bfloat16)
        for p in ps:
            send_on(p).start()

    def gradient(t, u):
        g = lax.dot_general(
            left_v[rows(t), :], picked(t), (((1,), (1,)), ((), ())), preferred_element_type=jnp.float32
        )
        for j in range(pairs):
            wide[u, pl.ds(j, TILE, stride=pairs), :] = g[:, j * TILE:(j + 1) * TILE]
        grad_v[mixed(t), :] = wide[u].astype(jnp.bfloat16)

    @pl.when(has_pre)
    def _():
        for u in range(REACH):
            arrive(-1 - u)

        @pl.when(wider)
        def _():
            for u in range(REACH, EDGE):
                arrive(-1 - u)

    for u in range(REACH):
        take(u)

    def halo_ready(hs):
        for h in hs:
            pltpu.make_async_copy(halo_a.at[h], halo_a.at[h], halo_sem.at[h]).wait()

    @pl.when(jnp.logical_and(wider, has_pre))
    def _():
        halo_ready((0, 1))
        halo_tiles((-2, -1), (1, 0))

    sends_edges = jnp.logical_and(col > 0, jnp.logical_not(wider))
    out_reach = jnp.where(first, REACH, EDGE)

    def step(p, carry):
        t = local(p)

        @pl.when(jnp.logical_and(first, p % GROUP == 0))
        def _():
            sort_group(p // GROUP)

        @pl.when(p + REACH < tiles)
        def _():
            take(p + REACH)

        @pl.when(jnp.logical_and(p + REACH >= tiles, has_post))
        def _():
            arrive(p + REACH)

        acc = jnp.dot(a_v[rows(t), :], picked(t), preferred_element_type=jnp.float32)
        fresh[t + REACH] = acc.astype(jnp.bfloat16)

        @pl.when(col > 0)
        def _():
            @pl.when(jnp.logical_and(jnp.logical_and(p < out_reach, has_pre), sends_edges))
            def _():
                send_pre(held(p), p, col - 1, 0).start()

            send_on(p).start()

            @pl.when(jnp.logical_and(jnp.logical_and(p >= tiles - out_reach, has_post), sends_edges))
            def _():
                send_post(held(p), p, col - 1, 0).start()

        @pl.when(jnp.logical_and(col == 0, t % 2 == 1))
        def _():
            gradient(t, 0)

        return carry

    lax.fori_loop(0, tiles, step, 0)

    @pl.when(jnp.logical_and(wider, has_post))
    def _():
        arrive(tiles + REACH)
        arrive(tiles + REACH + 1)
        halo_ready((2, 3))
        halo_tiles((tiles, tiles + 1), (2, 3))

    store_env.start()

    @pl.when(col > 0)
    def _():
        def two(i, carry):
            gradient(2 * i, 0)
            gradient(2 * i + 1, 1)
            store_grad(i).start()
            return carry

        lax.fori_loop(0, tiles // 2, two, 0)

    @pl.when(col == 0)
    def _():
        def two(i, carry):
            gradient(4 * i, 0)
            gradient(4 * i + 2, 1)
            store_grad(2 * i).start()
            store_grad(2 * i + 1).start()
            return carry

        lax.fori_loop(0, tiles // 4, two, 0)

    @pl.when(col > 0)
    def _():
        def sent(p, carry):
            send_on(p).wait_send()
            return carry

        lax.fori_loop(0, tiles, sent, 0)

    for there, at in ((has_pre, -REACH), (has_post, tiles)):
        @pl.when(jnp.logical_and(wider, there))
        def _():
            for u in range(REACH):
                send_on(at + u).wait_send()

    edge_spreads(lambda p, copy: copy.wait_send())

    for u in range(EDGE):
        sent_edge = jnp.logical_and(sends_edges, u < out_reach)

        @pl.when(jnp.logical_and(sent_edge, has_pre))
        def _():
            send_pre(held(u), u, col - 1, 0).wait_send()

        @pl.when(jnp.logical_and(sent_edge, has_post))
        def _():
            send_post(held(tiles - 1 - u), tiles - 1 - u, col - 1, 0).wait_send()

    first_edges(lambda copy: copy.wait_send())
    store_env.wait()

    def stored(i, carry):
        store_grad(i).wait()
        return carry

    lax.fori_loop(0, tiles // 2, stored, 0)


def per_device(env_right, transfer, sources, env_left):
    ncol = lax.axis_size("col")
    nsec = lax.axis_size("sec")
    length = transfer.shape[2]
    pairs = transfer.shape[3]
    width = env_right.shape[2]
    tiles = length // TILE
    b = transfer.reshape(length * pairs, TILE)
    left = env_left.reshape(length, width)
    src = jnp.transpose(sources.reshape(tiles, pairs))
    bf16 = jnp.bfloat16
    in_hbm = pl.BlockSpec(memory_space=pltpu.HBM)
    anywhere = pl.BlockSpec(memory_space=pl.ANY)
    dma = pltpu.SemaphoreType.DMA
    env, grad = pl.pallas_call(
        functools.partial(sweep_kernel, ncol, nsec, pairs),
        out_shape=(
            jax.ShapeDtypeStruct((tiles, TILE, width), bf16),
            jax.ShapeDtypeStruct((length * pairs, TILE), bf16),
        ),
        in_specs=[pl.BlockSpec(memory_space=pltpu.SMEM), in_hbm, in_hbm, in_hbm],
        out_specs=(anywhere, anywhere),
        scratch_shapes=[
            pltpu.VMEM((length * pairs, TILE), bf16),
            pltpu.VMEM((length, pairs * TILE), bf16),
            pltpu.VMEM((length, width), bf16),
            pltpu.VMEM((length, width), bf16),
            pltpu.VMEM((tiles + 2 * EDGE, TILE, width), bf16),
            pltpu.VMEM((tiles + 2 * EDGE, TILE, width), bf16),
            pltpu.VMEM((tiles + 2 * REACH, TILE, width), bf16),
            pltpu.VMEM((length * pairs, TILE), bf16),
            pltpu.VMEM((2, pairs * TILE, TILE), jnp.float32),
            pltpu.VMEM((2 * REACH, TILE, (2 * REACH + 1) * TILE), bf16),
            pltpu.VMEM((2 * REACH, TILE, (2 * REACH + 1) * TILE), bf16),
            dma((tiles + 2 * EDGE,)),
            dma((tiles + 2 * REACH + 4 * EDGE,)),
            dma((tiles // GROUP,)),
            dma,
            dma,
            dma,
            dma((tiles // 2,)),
            dma((2 * REACH,)),
            dma((2 * REACH,)),
        ],
        compiler_params=pltpu.CompilerParams(
            collective_id=0, has_side_effects=True, vmem_limit_bytes=24 * 1024 * 1024
        ),
        name="sweep",
    )(src, *(pltpu.with_memory_space_constraint(x, pltpu.HBM) for x in (env_right.reshape(length, width), b, left)))
    return env.reshape(1, 1, length, width), grad.reshape(1, 1, length, pairs, TILE)


def solution(mesh):
    placed = (
        P(None, "sec", None),
        P("col", None, "sec", None, None),
        P("col", None, "sec", None),
        P("col", None, "sec", None),
    )
    return jax.shard_map(
        per_device,
        mesh=mesh,
        in_specs=placed,
        out_specs=(P("col", None, "sec", None), P("col", None, "sec", None, None)),
        check_vma=False,
    )
```

time: 106 us -> 93.3 us (0.88)
  Pallas kernels: 102 us -> 87.9 us
    pallas_call x1, Pallas kernels: 102 us -> 87.9 us  [per_device(): pl.pallas_call(functools.partial(sweep_kernel, ncol, nsec, pairs), out_sh...]
where the time goes in v3:
time: 93.3 us; the launch traced here: 92.2 us
  Pallas kernels  87.9 us (94%)
  local copies, waits for them, and re-layouts  3.66 us (4%)
    pallas_call x1, Pallas kernels, per_device(): pl.pallas_call(functools.partial(sweep_kernel, ncol, nsec, pairs), out_sh...  87.9 us
    unnamed x4, local copies, waits for them, and re-layouts  3.66 us

profile of v3, /device:TPU:24, one launch (start us, length us, event | category | flops | bytes accessed | tf_op | source)
XLA Modules:
  0.0 92.2 jit_solution(8929569326472271605)
XLA Ops:
  0.6 0.0 copy-start
  0.6 0.7 copy-done
  1.3 87.9 %sweep.1 = (bf16[32,128,128]{2,1,0:T(8,128)(2,1)S(1)}, bf16[16384,128]{1,0:T(8,128)(2,1)S(1)}) custom-call(s32[4,32]{1,0:T(4,128)S(1)} %bitcast.10, bf16[4096,128]{1,0:T(8,128)(2,1)} %bitcast.12, bf16[16384,128]{1,0:T(8,128)(2,1)} %bitcast.11, bf16[4096,128]{1,0:T(8,128)(2,1)} %bitcast.13), custom_call_target="tpu_custom_call" | custom-call | tf_op jit(solution)/shard_map/sweep/pallas_call | solution.py:390
  89.2 1.0 %copy.8 = bf16[1,1,4096,128]{3,2,1,0:T(8,128)(2,1)} copy(bf16[1,1,4096,128]{3,2,1,0:T(8,128)(2,1)S(1)} %bitcast.9) | data formatting | bytes 2097152
  90.2 2.0 %copy.9 = bf16[1,1,4096,4,128]{4,3,2,1,0:T(4,128)(2,1)} copy(bf16[1,1,4096,4,128]{4,3,2,1,0:T(4,128)(2,1)S(1)} %bitcast.8) | data formatting | bytes 8388608
Async XLA Ops:
  0.6 0.7 copy-start

commit v4 on v3

--- a/solution.py
+++ b/solution.py
@@ -23,7 +23,7 @@
     sec = lax.axis_index("sec")
     tiles = left_v.shape[0] // TILE
     groups = tiles // GROUP
-    odd = sec % 2
+    odd = 1 - sec % 2
     first = col == ncol - 1
     wider = jnp.logical_and(col % 2 == 1, jnp.logical_not(first))
     has_below = sec > 0
@@ -232,8 +232,6 @@
             near = win[pl.ds(w - REACH, 2 * REACH + 1)].reshape((2 * REACH + 1) * TILE, TILE)
             acc = jnp.dot(halo_a[h], near, preferred_element_type=jnp.float32)
             fresh[local(p) + REACH] = acc.astype(jnp.bfloat16)
-        for p in ps:
-            send_on(p).start()
 
     def gradient(t, u):
         g = lax.dot_general(
@@ -260,13 +258,36 @@
         for h in hs:
             pltpu.make_async_copy(halo_a.at[h], halo_a.at[h], halo_sem.at[h]).wait()
 
-    @pl.when(jnp.logical_and(wider, has_pre))
-    def _():
+    sends_edges = jnp.logical_and(col > 0, jnp.logical_not(wider))
+    out_reach = jnp.where(first, REACH, EDGE)
+
+    def own_tile(t):
+        acc = jnp.dot(a_v[rows(t), :], picked(t), preferred_element_type=jnp.float32)
+        fresh[t + REACH] = acc.astype(jnp.bfloat16)
+
+    def pass_on(p):
+        @pl.when(jnp.logical_and(jnp.logical_and(p < out_reach, has_pre), sends_edges))
+        def _():
+            send_pre(held(p), p, col - 1, 0).start()
+
+        @pl.when(col > 0)
+        def _():
+            send_on(p).start()
+
+        @pl.when(jnp.logical_and(jnp.logical_and(p >= tiles - out_reach, has_post), sends_edges))
+        def _():
+            send_post(held(p), p, col - 1, 0).start()
+
+    early = jnp.logical_and(wider, has_pre)
+
+    @pl.when(early)
+    def _():
+        take(REACH)
         halo_ready((0, 1))
         halo_tiles((-2, -1), (1, 0))
-
-    sends_edges = jnp.logical_and(col > 0, jnp.logical_not(wider))
-    out_reach = jnp.where(first, REACH, EDGE)
+        own_tile(local(0))
+        for p in (-2, -1, 0):
+            send_on(p).start()
 
     def step(p, carry):
         t = local(p)
@@ -283,20 +304,8 @@
         def _():
             arrive(p + REACH)
 
-        acc = jnp.dot(a_v[rows(t), :], picked(t), preferred_element_type=jnp.float32)
-        fresh[t + REACH] = acc.astype(jnp.bfloat16)
-
-        @pl.when(col > 0)
-        def _():
-            @pl.when(jnp.logical_and(jnp.logical_and(p < out_reach, has_pre), sends_edges))
-            def _():
-                send_pre(held(p), p, col - 1, 0).start()
-
-            send_on(p).start()
-
-            @pl.when(jnp.logical_and(jnp.logical_and(p >= tiles - out_reach, has_post), sends_edges))
-            def _():
-                send_post(held(p), p, col - 1, 0).start()
+        own_tile(t)
+        pass_on(p)
 
         @pl.when(jnp.logical_and(col == 0, t % 2 == 1))
         def _():
@@ -304,7 +313,7 @@
 
         return carry
 
-    lax.fori_loop(0, tiles, step, 0)
+    lax.fori_loop(count(early), tiles, step, 0)
 
     @pl.when(jnp.logical_and(wider, has_post))
     def _():
@@ -312,6 +321,8 @@
         arrive(tiles + REACH + 1)
         halo_ready((2, 3))
         halo_tiles((tiles, tiles + 1), (2, 3))
+        for p in (tiles, tiles + 1):
+            send_on(p).start()
 
     store_env.start()
 

time: 93.3 us -> 89.3 us (0.957)
  Pallas kernels: 87.9 us -> 83.8 us
    pallas_call x1, Pallas kernels: 87.9 us -> 83.8 us  [per_device(): pl.pallas_call(functools.partial(sweep_kernel, ncol, nsec, pairs), out_sh...]
where the time goes in v4:
time: 89.3 us; the launch traced here: 88.1 us
  Pallas kernels  83.8 us (94%)
  local copies, waits for them, and re-layouts  3.66 us (4%)
    pallas_call x1, Pallas kernels, per_device(): pl.pallas_call(functools.partial(sweep_kernel, ncol, nsec, pairs), out_sh...  83.8 us
    unnamed x4, local copies, waits for them, and re-layouts  3.66 us

profile of v4, /device:TPU:24, one launch (start us, length us, event | category | flops | bytes accessed | tf_op | source)
XLA Modules:
  0.0 88.1 jit_solution(5163879646314049820)
XLA Ops:
  0.6 0.0 copy-start
  0.6 0.7 copy-done
  1.3 83.8 %sweep.1 = (bf16[32,128,128]{2,1,0:T(8,128)(2,1)S(1)}, bf16[16384,128]{1,0:T(8,128)(2,1)S(1)}) custom-call(s32[4,32]{1,0:T(4,128)S(1)} %bitcast.10, bf16[4096,128]{1,0:T(8,128)(2,1)} %bitcast.12, bf16[16384,128]{1,0:T(8,128)(2,1)} %bitcast.11, bf16[4096,128]{1,0:T(8,128)(2,1)} %bitcast.13), custom_call_target="tpu_custom_call" | custom-call | tf_op jit(solution)/shard_map/sweep/pallas_call | solution.py:401
  85.1 1.0 %copy.8 = bf16[1,1,4096,128]{3,2,1,0:T(8,128)(2,1)} copy(bf16[1,1,4096,128]{3,2,1,0:T(8,128)(2,1)S(1)} %bitcast.9) | data formatting | bytes 2097152
  86.1 2.0 %copy.9 = bf16[1,1,4096,4,128]{4,3,2,1,0:T(4,128)(2,1)} copy(bf16[1,1,4096,4,128]{4,3,2,1,0:T(4,128)(2,1)S(1)} %bitcast.8) | data formatting | bytes 8388608
Async XLA Ops:
  0.6 0.7 copy-start

commit v5 on v4

--- a/solution.py
+++ b/solution.py
@@ -56,7 +56,7 @@
     store_env = pltpu.make_async_copy(fresh.at[pl.ds(REACH, tiles)], env_out, out_sem)
 
     def store_grad(i):
-        span = mixed(2 * i, 2)
+        span = mixed(4 * i, 4)
         return pltpu.make_async_copy(grad_v.at[span], grad_out.at[span], gout_sem.at[i])
 
     def send(src, w, sem, to_col, to_sec):
@@ -72,10 +72,10 @@
     def held(p):
         return fresh.at[local(p) + REACH]
 
-    def send_on(p):
-        return send(held(p), slot(p), p + REACH, col - 1, sec)
-
-    after = tiles + 2 * REACH
+    def send_on(p, own=None):
+        return send(held(p), slot(p), REACH if own is None else own, col - 1, sec)
+
+    after = 2 * REACH + 1
 
     def send_pre(src, p, to_col, at):
         return send(src, slot_beside(-1 - p), after + at + p, to_col, sec + side)
@@ -270,15 +270,16 @@
         def _():
             send_pre(held(p), p, col - 1, 0).start()
 
+        @pl.when(jnp.logical_and(jnp.logical_and(p >= tiles - out_reach, has_post), sends_edges))
+        def _():
+            send_post(held(p), p, col - 1, 0).start()
+
         @pl.when(col > 0)
         def _():
             send_on(p).start()
 
-        @pl.when(jnp.logical_and(jnp.logical_and(p >= tiles - out_reach, has_post), sends_edges))
-        def _():
-            send_post(held(p), p, col - 1, 0).start()
-
     early = jnp.logical_and(wider, has_pre)
+    last = tiles - REACH
 
     @pl.when(early)
     def _():
@@ -286,8 +287,9 @@
         halo_ready((0, 1))
         halo_tiles((-2, -1), (1, 0))
         own_tile(local(0))
-        for p in (-2, -1, 0):
-            send_on(p).start()
+        send_on(-2, 0).start()
+        send_on(-1, 1).start()
+        send_on(0).start()
 
     def step(p, carry):
         t = local(p)
@@ -296,14 +298,7 @@
         def _():
             sort_group(p // GROUP)
 
-        @pl.when(p + REACH < tiles)
-        def _():
-            take(p + REACH)
-
-        @pl.when(jnp.logical_and(p + REACH >= tiles, has_post))
-        def _():
-            arrive(p + REACH)
-
+        take(p + REACH)
         own_tile(t)
         pass_on(p)
 
@@ -313,53 +308,70 @@
 
         return carry
 
-    lax.fori_loop(count(early), tiles, step, 0)
-
-    @pl.when(jnp.logical_and(wider, has_post))
-    def _():
-        arrive(tiles + REACH)
-        arrive(tiles + REACH + 1)
+    lax.fori_loop(count(early), last, step, 0)
+
+    @pl.when(has_post)
+    def _():
+        arrive(tiles)
+        arrive(tiles + 1)
+
+    late = jnp.logical_and(wider, has_post)
+
+    @pl.when(late)
+    def _():
+        arrive(tiles + 2)
+        arrive(tiles + 3)
         halo_ready((2, 3))
+        own_tile(local(last))
+        own_tile(local(last + 1))
         halo_tiles((tiles, tiles + 1), (2, 3))
-        for p in (tiles, tiles + 1):
-            send_on(p).start()
+        send_on(last).start()
+        send_on(last + 1).start()
+        send_on(tiles, 3).start()
+        send_on(tiles + 1, 4).start()
+
+    @pl.when(jnp.logical_not(late))
+    def _():
+        own_tile(local(last))
+        own_tile(local(last + 1))
+        pass_on(last)
+        pass_on(last + 1)
 
     store_env.start()
 
     @pl.when(col > 0)
     def _():
-        def two(i, carry):
-            gradient(2 * i, 0)
-            gradient(2 * i + 1, 1)
+        def four(i, carry):
+            for u in range(4):
+                gradient(4 * i + u, u)
             store_grad(i).start()
             return carry
 
-        lax.fori_loop(0, tiles // 2, two, 0)
+        lax.fori_loop(0, tiles // 4, four, 0)
 
     @pl.when(col == 0)
     def _():
-        def two(i, carry):
-            gradient(4 * i, 0)
-            gradient(4 * i + 2, 1)
+        gradient(local(last + 1 - odd), 0)
+
+        def four(i, carry):
+            for u in range(4):
+                gradient(8 * i + 2 * u, u)
             store_grad(2 * i).start()
             store_grad(2 * i + 1).start()
             return carry
 
-        lax.fori_loop(0, tiles // 4, two, 0)
+        lax.fori_loop(0, tiles // 8, four, 0)
 
     @pl.when(col > 0)
     def _():
-        def sent(p, carry):
-            send_on(p).wait_send()
-            return carry
-
-        lax.fori_loop(0, tiles, sent, 0)
-
-    for there, at in ((has_pre, -REACH), (has_post, tiles)):
+        main = fresh.at[pl.ds(REACH, tiles)]
+        pltpu.make_async_copy(main, main, send_sem.at[REACH]).wait()
+
+    for there, at, own in ((has_pre, -REACH, 0), (has_post, tiles, 3)):
         @pl.when(jnp.logical_and(wider, there))
         def _():
             for u in range(REACH):
-                send_on(at + u).wait_send()
+                send_on(at + u, own + u).wait_send()
 
     edge_spreads(lambda p, copy: copy.wait_send())
 
@@ -381,7 +393,7 @@
         store_grad(i).wait()
         return carry
 
-    lax.fori_loop(0, tiles // 2, stored, 0)
+    lax.fori_loop(0, tiles // 4, stored, 0)
 
 
 def per_device(env_right, transfer, sources, env_left):
@@ -415,16 +427,16 @@
             pltpu.VMEM((tiles + 2 * EDGE, TILE, width), bf16),
             pltpu.VMEM((tiles + 2 * REACH, TILE, width), bf16),
             pltpu.VMEM((length * pairs, TILE), bf16),
-            pltpu.VMEM((2, pairs * TILE, TILE), jnp.float32),
+            pltpu.VMEM((4, pairs * TILE, TILE), jnp.float32),
             pltpu.VMEM((2 * REACH, TILE, (2 * REACH + 1) * TILE), bf16),
             pltpu.VMEM((2 * REACH, TILE, (2 * REACH + 1) * TILE), bf16),
             dma((tiles + 2 * EDGE,)),
-            dma((tiles + 2 * REACH + 4 * EDGE,)),
+            dma((2 * REACH + 1 + 4 * EDGE,)),
             dma((tiles // GROUP,)),
             dma,
             dma,
             dma,
-            dma((tiles // 2,)),
+            dma((tiles // 4,)),
             dma((2 * REACH,)),
             dma((2 * REACH,)),
         ],

time: 89.3 us -> 85.6 us (0.959); the launches traced: 88.1 us -> 85.5 us
  Pallas kernels: 83.8 us -> 81.2 us
    pallas_call x1, Pallas kernels: 83.8 us -> 81.2 us  [per_device(): pl.pallas_call(functools.partial(sweep_kernel, ncol, nsec, pairs), out_sh...]
where the time goes in v5:
time: 85.6 us; the launch traced here: 85.5 us
  Pallas kernels  81.2 us (95%)
  local copies, waits for them, and re-layouts  3.66 us (4%)
    pallas_call x1, Pallas kernels, per_device(): pl.pallas_call(functools.partial(sweep_kernel, ncol, nsec, pairs), out_sh...  81.2 us
    unnamed x4, local copies, waits for them, and re-layouts  3.66 us

profile of v5, /device:TPU:24, one launch (start us, length us, event | category | flops | bytes accessed | tf_op | source)
XLA Modules:
  0.0 85.5 jit_solution(5188521871488874393)
XLA Ops:
  0.6 0.0 copy-start
  0.6 0.7 copy-done
  1.3 81.2 %sweep.1 = (bf16[32,128,128]{2,1,0:T(8,128)(2,1)S(1)}, bf16[16384,128]{1,0:T(8,128)(2,1)S(1)}) custom-call(s32[4,32]{1,0:T(4,128)S(1)} %bitcast.10, bf16[4096,128]{1,0:T(8,128)(2,1)} %bitcast.12, bf16[16384,128]{1,0:T(8,128)(2,1)} %bitcast.11, bf16[4096,128]{1,0:T(8,128)(2,1)} %bitcast.13), custom_call_target="tpu_custom_call" | custom-call | tf_op jit(solution)/shard_map/sweep/pallas_call | solution.py:413
  82.5 1.0 %copy.8 = bf16[1,1,4096,128]{3,2,1,0:T(8,128)(2,1)} copy(bf16[1,1,4096,128]{3,2,1,0:T(8,128)(2,1)S(1)} %bitcast.9) | data formatting | bytes 2097152
  83.5 2.0 %copy.9 = bf16[1,1,4096,4,128]{4,3,2,1,0:T(4,128)(2,1)} copy(bf16[1,1,4096,4,128]{4,3,2,1,0:T(4,128)(2,1)S(1)} %bitcast.8) | data formatting | bytes 8388608
Async XLA Ops:
  0.6 0.7 copy-start

commit v6 on v5

--- a/solution.py
+++ b/solution.py
@@ -15,9 +15,9 @@
 
 
 def sweep_kernel(
-    ncol, nsec, pairs, src_ref, env_hbm, b_hbm, left_hbm, env_out, grad_out,
-    b_v, a_v, left_v, env_v, land, win, fresh, grad_v, wide, spread, halo_a,
-    recv_sem, send_sem, b_sem, left_sem, env_sem, out_sem, gout_sem, spread_sem, halo_sem,
+    ncol, nsec, pairs, src_hbm, env_hbm, b_hbm, left_hbm, env_out, grad_out,
+    src_ref, b_v, a_v, left_v, env_v, land, win, fresh, grad_v, wide, spread, halo_a,
+    src_sem, recv_sem, send_sem, b_sem, left_sem, env_sem, out_sem, gout_sem, spread_sem, halo_sem,
 ):
     col = lax.axis_index("col")
     sec = lax.axis_index("sec")
@@ -51,6 +51,7 @@
         span = mixed(g * GROUP, GROUP)
         return pltpu.make_async_copy(b_hbm.at[span], b_v.at[span], b_sem.at[g])
 
+    load_src = pltpu.make_async_copy(src_hbm, src_ref, src_sem)
     load_left = pltpu.make_async_copy(left_hbm, left_v, left_sem)
     load_env = pltpu.make_async_copy(env_hbm, env_v, env_sem)
     store_env = pltpu.make_async_copy(fresh.at[pl.ds(REACH, tiles)], env_out, out_sem)
@@ -113,6 +114,8 @@
         def _():
             greet(col, sec + by)
 
+    load_src.start()
+
     @pl.when(first)
     def _():
         load_env.start()
@@ -147,6 +150,7 @@
 
     first_edges(lambda copy: copy.start())
     win[...] = jnp.zeros_like(win)
+    load_src.wait()
 
     def sort_rows(t):
         wide[0] = b_v[mixed(t), :].astype(jnp.float32)
@@ -209,15 +213,11 @@
     def take(p):
         @pl.when(first)
         def _():
-            win[slot(p)] = env_v[rows(local(p)), :]
+            from_start(p)
 
         @pl.when(jnp.logical_not(first))
         def _():
             arrive(p)
-
-    @pl.when(first)
-    def _():
-        load_env.wait()
 
     def picked(t):
         parts = []
@@ -241,6 +241,22 @@
             wide[u, pl.ds(j, TILE, stride=pairs), :] = g[:, j * TILE:(j + 1) * TILE]
         grad_v[mixed(t), :] = wide[u].astype(jnp.bfloat16)
 
+    def own_tile(t):
+        acc = jnp.dot(a_v[rows(t), :], picked(t), preferred_element_type=jnp.float32)
+        fresh[t + REACH] = acc.astype(jnp.bfloat16)
+
+    def from_start(p):
+        win[slot(p)] = env_v[rows(local(p)), :]
+
+    @pl.when(first)
+    def _():
+        load_env.wait()
+        sort_group(0)
+        for p in range(GROUP + REACH):
+            from_start(p)
+        for p in range(REACH, GROUP):
+            own_tile(local(p))
+
     @pl.when(has_pre)
     def _():
         for u in range(REACH):
@@ -251,8 +267,10 @@
             for u in range(REACH, EDGE):
                 arrive(-1 - u)
 
-    for u in range(REACH):
-        take(u)
+    @pl.when(jnp.logical_not(first))
+    def _():
+        for u in range(REACH):
+            arrive(u)
 
     def halo_ready(hs):
         for h in hs:
@@ -261,9 +279,8 @@
     sends_edges = jnp.logical_and(col > 0, jnp.logical_not(wider))
     out_reach = jnp.where(first, REACH, EDGE)
 
-    def own_tile(t):
-        acc = jnp.dot(a_v[rows(t), :], picked(t), preferred_element_type=jnp.float32)
-        fresh[t + REACH] = acc.astype(jnp.bfloat16)
+    ahead_pre = jnp.logical_and(jnp.logical_and(sends_edges, has_pre), jnp.logical_not(first))
+    ahead_post = jnp.logical_and(jnp.logical_and(sends_edges, has_post), jnp.logical_not(first))
 
     def pass_on(p):
         @pl.when(jnp.logical_and(jnp.logical_and(p < out_reach, has_pre), sends_edges))
@@ -274,16 +291,32 @@
         def _():
             send_post(held(p), p, col - 1, 0).start()
 
-        @pl.when(col > 0)
+        behind_pre = jnp.logical_and(ahead_pre, p < EDGE)
+        behind_post = jnp.logical_and(ahead_post, p >= tiles - EDGE)
+
+        @pl.when(jnp.logical_or(jnp.logical_and(behind_pre, p > 0), jnp.logical_and(behind_post, p > tiles - EDGE)))
+        def _():
+            send_on(p - 1).start()
+
+        held_back = jnp.logical_or(jnp.logical_and(behind_pre, p < EDGE - 1), jnp.logical_and(behind_post, p < tiles - 1))
+
+        @pl.when(jnp.logical_and(col > 0, jnp.logical_not(held_back)))
         def _():
             send_on(p).start()
 
     early = jnp.logical_and(wider, has_pre)
     last = tiles - REACH
 
+    @pl.when(first)
+    def _():
+        for p in range(REACH):
+            own_tile(local(p))
+        for p in range(GROUP):
+            pass_on(p)
+
     @pl.when(early)
     def _():
-        take(REACH)
+        arrive(REACH)
         halo_ready((0, 1))
         halo_tiles((-2, -1), (1, 0))
         own_tile(local(0))
@@ -308,7 +341,7 @@
 
         return carry
 
-    lax.fori_loop(count(early), last, step, 0)
+    lax.fori_loop(count(early) + GROUP * count(first), last, step, 0)
 
     @pl.when(has_post)
     def _():
@@ -334,8 +367,18 @@
     def _():
         own_tile(local(last))
         own_tile(local(last + 1))
-        pass_on(last)
-        pass_on(last + 1)
+
+        @pl.when(ahead_post)
+        def _():
+            send_post(held(last), last, col - 1, 0).start()
+            send_post(held(last + 1), last + 1, col - 1, 0).start()
+            for p in range(last - 1, tiles):
+                send_on(p).start()
+
+        @pl.when(jnp.logical_not(ahead_post))
+        def _():
+            pass_on(last)
+            pass_on(last + 1)
 
     store_env.start()
 
@@ -416,9 +459,10 @@
             jax.ShapeDtypeStruct((tiles, TILE, width), bf16),
             jax.ShapeDtypeStruct((length * pairs, TILE), bf16),
         ),
-        in_specs=[pl.BlockSpec(memory_space=pltpu.SMEM), in_hbm, in_hbm, in_hbm],
+        in_specs=[in_hbm, in_hbm, in_hbm, in_hbm],
         out_specs=(anywhere, anywhere),
         scratch_shapes=[
+            pltpu.SMEM((pairs, tiles), jnp.int32),
             pltpu.VMEM((length * pairs, TILE), bf16),
             pltpu.VMEM((length, pairs * TILE), bf16),
             pltpu.VMEM((length, width), bf16),
@@ -430,6 +474,7 @@
             pltpu.VMEM((4, pairs * TILE, TILE), jnp.float32),
             pltpu.VMEM((2 * REACH, TILE, (2 * REACH + 1) * TILE), bf16),
             pltpu.VMEM((2 * REACH, TILE, (2 * REACH + 1) * TILE), bf16),
+            dma,
             dma((tiles + 2 * EDGE,)),
             dma((2 * REACH + 1 + 4 * EDGE,)),
             dma((tiles // GROUP,)),
@@ -444,7 +489,7 @@
             collective_id=0, has_side_effects=True, vmem_limit_bytes=24 * 1024 * 1024
         ),
         name="sweep",
-    )(src, *(pltpu.with_memory_space_constraint(x, pltpu.HBM) for x in (env_right.reshape(length, width), b, left)))
+    )(*(pltpu.with_memory_space_constraint(x, pltpu.HBM) for x in (src, env_right.reshape(length, width), b, left)))
     return env.reshape(1, 1, length, width), grad.reshape(1, 1, length, pairs, TILE)
 
 

time: 85.6 us -> 80.2 us (0.937)
  Pallas kernels: 81.2 us -> 76.5 us
    pallas_call x1, Pallas kernels: 81.2 us -> 76.5 us  [per_device(): pl.pallas_call(functools.partial(sweep_kernel, ncol, nsec, pairs), out_sh...]
    unnamed x4 -> x2, local copies, waits for them, and re-layouts: 3.66 us -> 2.99 us
where the time goes in v6:
time: 80.2 us; the launch traced here: 80.1 us
  Pallas kernels  76.5 us (95%)
  local copies, waits for them, and re-layouts  2.99 us (4%)
    pallas_call x1, Pallas kernels, per_device(): pl.pallas_call(functools.partial(sweep_kernel, ncol, nsec, pairs), out_sh...  76.5 us
    unnamed x2, local copies, waits for them, and re-layouts  2.99 us

profile of v6, /device:TPU:24, one launch (start us, length us, event | category | flops | bytes accessed | tf_op | source)
XLA Modules:
  0.0 80.1 jit_solution(10159391293100167283)
XLA Ops:
  0.6 76.5 %sweep.1 = (bf16[32,128,128]{2,1,0:T(8,128)(2,1)S(1)}, bf16[16384,128]{1,0:T(8,128)(2,1)S(1)}) custom-call(s32[4,32]{1,0:T(4,128)} %bitcast.13, bf16[4096,128]{1,0:T(8,128)(2,1)} %bitcast.11, bf16[16384,128]{1,0:T(8,128)(2,1)} %bitcast.10, bf16[4096,128]{1,0:T(8,128)(2,1)} %bitcast.12), custom_call_target="tpu_custom_call" | custom-call | tf_op jit(solution)/shard_map/sweep/pallas_call | solution.py:456
  77.1 1.0 %copy.8 = bf16[1,1,4096,128]{3,2,1,0:T(8,128)(2,1)} copy(bf16[1,1,4096,128]{3,2,1,0:T(8,128)(2,1)S(1)} %bitcast.9) | data formatting | bytes 2097152
  78.1 2.0 %copy.9 = bf16[1,1,4096,4,128]{4,3,2,1,0:T(4,128)(2,1)} copy(bf16[1,1,4096,4,128]{4,3,2,1,0:T(4,128)(2,1)S(1)} %bitcast.8) | data formatting | bytes 8388608

commit v7 on v6

--- a/solution.py
+++ b/solution.py
@@ -11,6 +11,7 @@
 REACH = 2
 EDGE = 2 * REACH
 GROUP = 4
+EARLY = 3
 MESH = pl.DeviceIdType.MESH
 
 
@@ -323,6 +324,14 @@
         send_on(-2, 0).start()
         send_on(-1, 1).start()
         send_on(0).start()
+        arrive(REACH + 1)
+        arrive(REACH + 2)
+        own_tile(local(1))
+        own_tile(local(2))
+        send_on(1).start()
+        send_on(2).start()
+
+    nearby = col < 2
 
     def step(p, carry):
         t = local(p)
@@ -332,16 +341,24 @@
             sort_group(p // GROUP)
 
         take(p + REACH)
-        own_tile(t)
+        @pl.when(nearby)
+        def _():
+            own_tile(t)
+            gradient(t, 0)
+
+        @pl.when(jnp.logical_not(nearby))
+        def _():
+            own_tile(t)
+
         pass_on(p)
 
-        @pl.when(jnp.logical_and(col == 0, t % 2 == 1))
-        def _():
-            gradient(t, 0)
+        @pl.when(jnp.logical_and(jnp.logical_and(nearby, p % GROUP == GROUP - 1), p >= GROUP))
+        def _():
+            store_grad(t // GROUP).start()
 
         return carry
 
-    lax.fori_loop(count(early) + GROUP * count(first), last, step, 0)
+    lax.fori_loop(EARLY * count(early) + GROUP * count(first), last, step, 0)
 
     @pl.when(has_post)
     def _():
@@ -382,28 +399,24 @@
 
     store_env.start()
 
-    @pl.when(col > 0)
+    @pl.when(jnp.logical_not(nearby))
     def _():
         def four(i, carry):
-            for u in range(4):
-                gradient(4 * i + u, u)
+            for u in range(GROUP):
+                gradient(GROUP * i + u, u)
             store_grad(i).start()
             return carry
 
-        lax.fori_loop(0, tiles // 4, four, 0)
-
-    @pl.when(col == 0)
-    def _():
-        gradient(local(last + 1 - odd), 0)
-
-        def four(i, carry):
-            for u in range(4):
-                gradient(8 * i + 2 * u, u)
-            store_grad(2 * i).start()
-            store_grad(2 * i + 1).start()
-            return carry
-
-        lax.fori_loop(0, tiles // 8, four, 0)
+        lax.fori_loop(0, groups, four, 0)
+
+    @pl.when(nearby)
+    def _():
+        for u in range(EARLY):
+            gradient(local(u), u)
+        store_grad(local(0) // GROUP).start()
+        for u in range(REACH):
+            gradient(local(last + u), u)
+        store_grad(local(last) // GROUP).start()
 
     @pl.when(col > 0)
     def _():

time: 80.2 us -> 79.1 us (0.986)
  Pallas kernels: 76.5 us -> 75.3 us
    pallas_call x1, Pallas kernels: 76.5 us -> 75.3 us  [per_device(): pl.pallas_call(functools.partial(sweep_kernel, ncol, nsec, pairs), out_sh...]
where the time goes in v7:
time: 79.1 us; the launch traced here: 79 us
  Pallas kernels  75.3 us (95%)
  local copies, waits for them, and re-layouts  2.99 us (4%)
    pallas_call x1, Pallas kernels, per_device(): pl.pallas_call(functools.partial(sweep_kernel, ncol, nsec, pairs), out_sh...  75.3 us
    unnamed x2, local copies, waits for them, and re-layouts  2.99 us

profile of v7, /device:TPU:24, one launch (start us, length us, event | category | flops | bytes accessed | tf_op | source)
XLA Modules:
  0.0 79.0 jit_solution(14152133576367129888)
XLA Ops:
  0.6 75.3 %sweep.1 = (bf16[32,128,128]{2,1,0:T(8,128)(2,1)S(1)}, bf16[16384,128]{1,0:T(8,128)(2,1)S(1)}) custom-call(s32[4,32]{1,0:T(4,128)} %bitcast.13, bf16[4096,128]{1,0:T(8,128)(2,1)} %bitcast.11, bf16[16384,128]{1,0:T(8,128)(2,1)} %bitcast.10, bf16[4096,128]{1,0:T(8,128)(2,1)} %bitcast.12), custom_call_target="tpu_custom_call" | custom-call | tf_op jit(solution)/shard_map/sweep/pallas_call | solution.py:469
  76.0 1.0 %copy.8 = bf16[1,1,4096,128]{3,2,1,0:T(8,128)(2,1)} copy(bf16[1,1,4096,128]{3,2,1,0:T(8,128)(2,1)S(1)} %bitcast.9) | data formatting | bytes 2097152
  77.0 2.0 %copy.9 = bf16[1,1,4096,4,128]{4,3,2,1,0:T(4,128)(2,1)} copy(bf16[1,1,4096,4,128]{4,3,2,1,0:T(4,128)(2,1)S(1)} %bitcast.8) | data formatting | bytes 8388608

commit v8 on v7

--- a/solution.py
+++ b/solution.py
@@ -295,11 +295,11 @@
         behind_pre = jnp.logical_and(ahead_pre, p < EDGE)
         behind_post = jnp.logical_and(ahead_post, p >= tiles - EDGE)
 
-        @pl.when(jnp.logical_or(jnp.logical_and(behind_pre, p > 0), jnp.logical_and(behind_post, p > tiles - EDGE)))
+        @pl.when(jnp.logical_and(behind_pre, p > 0))
         def _():
             send_on(p - 1).start()
 
-        held_back = jnp.logical_or(jnp.logical_and(behind_pre, p < EDGE - 1), jnp.logical_and(behind_post, p < tiles - 1))
+        held_back = jnp.logical_or(jnp.logical_and(behind_pre, p < EDGE - 1), behind_post)
 
         @pl.when(jnp.logical_and(col > 0, jnp.logical_not(held_back)))
         def _():
@@ -389,7 +389,7 @@
         def _():
             send_post(held(last), last, col - 1, 0).start()
             send_post(held(last + 1), last + 1, col - 1, 0).start()
-            for p in range(last - 1, tiles):
+            for p in range(tiles - EDGE, tiles):
                 send_on(p).start()
 
         @pl.when(jnp.logical_not(ahead_post))

time: 79.1 us -> 78.1 us (0.987)
  Pallas kernels: 75.3 us -> 74.3 us
    pallas_call x1, Pallas kernels: 75.3 us -> 74.3 us  [per_device(): pl.pallas_call(functools.partial(sweep_kernel, ncol, nsec, pairs), out_sh...]
where the time goes in v8:
time: 78.1 us; the launch traced here: 78 us
  Pallas kernels  74.3 us (95%)
  local copies, waits for them, and re-layouts  2.99 us (4%)
    pallas_call x1, Pallas kernels, per_device(): pl.pallas_call(functools.partial(sweep_kernel, ncol, nsec, pairs), out_sh...  74.3 us
    unnamed x2, local copies, waits for them, and re-layouts  2.99 us

profile of v8, /device:TPU:24, one launch (start us, length us, event | category | flops | bytes accessed | tf_op | source)
XLA Modules:
  0.0 78.0 jit_solution(8997647893688776532)
XLA Ops:
  0.6 74.3 %sweep.1 = (bf16[32,128,128]{2,1,0:T(8,128)(2,1)S(1)}, bf16[16384,128]{1,0:T(8,128)(2,1)S(1)}) custom-call(s32[4,32]{1,0:T(4,128)} %bitcast.13, bf16[4096,128]{1,0:T(8,128)(2,1)} %bitcast.11, bf16[16384,128]{1,0:T(8,128)(2,1)} %bitcast.10, bf16[4096,128]{1,0:T(8,128)(2,1)} %bitcast.12), custom_call_target="tpu_custom_call" | custom-call | tf_op jit(solution)/shard_map/sweep/pallas_call | solution.py:469
  75.0 1.0 %copy.8 = bf16[1,1,4096,128]{3,2,1,0:T(8,128)(2,1)} copy(bf16[1,1,4096,128]{3,2,1,0:T(8,128)(2,1)S(1)} %bitcast.9) | data formatting | bytes 2097152
  75.9 2.0 %copy.9 = bf16[1,1,4096,4,128]{4,3,2,1,0:T(4,128)(2,1)} copy(bf16[1,1,4096,4,128]{4,3,2,1,0:T(4,128)(2,1)S(1)} %bitcast.8) | data formatting | bytes 8388608

commit v9 on v8

--- a/solution.py
+++ b/solution.py
@@ -283,25 +283,32 @@
     ahead_pre = jnp.logical_and(jnp.logical_and(sends_edges, has_pre), jnp.logical_not(first))
     ahead_post = jnp.logical_and(jnp.logical_and(sends_edges, has_post), jnp.logical_not(first))
 
-    def pass_on(p):
-        @pl.when(jnp.logical_and(jnp.logical_and(p < out_reach, has_pre), sends_edges))
-        def _():
-            send_pre(held(p), p, col - 1, 0).start()
-
-        @pl.when(jnp.logical_and(jnp.logical_and(p >= tiles - out_reach, has_post), sends_edges))
-        def _():
-            send_post(held(p), p, col - 1, 0).start()
-
-        behind_pre = jnp.logical_and(ahead_pre, p < EDGE)
-        behind_post = jnp.logical_and(ahead_post, p >= tiles - EDGE)
-
-        @pl.when(jnp.logical_and(behind_pre, p > 0))
-        def _():
-            send_on(p - 1).start()
-
-        held_back = jnp.logical_or(jnp.logical_and(behind_pre, p < EDGE - 1), behind_post)
-
-        @pl.when(jnp.logical_and(col > 0, jnp.logical_not(held_back)))
+    forward = col > 0
+
+    def pass_on(p, kind):
+        if kind == "first":
+            if p < REACH:
+                @pl.when(has_pre)
+                def _():
+                    send_pre(held(p), p, col - 1, 0).start()
+
+            send_on(p).start()
+            return
+        before = p < EDGE
+        ahead = ahead_pre if before else ahead_post
+
+        @pl.when(ahead)
+        def _():
+            if before:
+                send_pre(held(p), p, col - 1, 0).start()
+                if p > 0:
+                    send_on(p - 1).start()
+                if p == EDGE - 1:
+                    send_on(p).start()
+            else:
+                send_post(held(p), p, col - 1, 0).start()
+
+        @pl.when(jnp.logical_and(forward, jnp.logical_not(ahead)))
         def _():
             send_on(p).start()
 
@@ -313,7 +320,7 @@
         for p in range(REACH):
             own_tile(local(p))
         for p in range(GROUP):
-            pass_on(p)
+            pass_on(p, "first")
 
     @pl.when(early)
     def _():
@@ -333,32 +340,67 @@
 
     nearby = col < 2
 
-    def step(p, carry):
-        t = local(p)
-
-        @pl.when(jnp.logical_and(first, p % GROUP == 0))
-        def _():
-            sort_group(p // GROUP)
-
-        take(p + REACH)
-        @pl.when(nearby)
-        def _():
-            own_tile(t)
-            gradient(t, 0)
-
-        @pl.when(jnp.logical_not(nearby))
-        def _():
-            own_tile(t)
-
-        pass_on(p)
-
-        @pl.when(jnp.logical_and(jnp.logical_and(nearby, p % GROUP == GROUP - 1), p >= GROUP))
-        def _():
-            store_grad(t // GROUP).start()
-
-        return carry
-
-    lax.fori_loop(EARLY * count(early) + GROUP * count(first), last, step, 0)
+    def advance(p, kind):
+        if kind == "first":
+            from_start(p + REACH)
+        else:
+            arrive(p + REACH)
+        own_tile(local(p))
+        if kind == "near":
+            gradient(local(p), 0)
+
+    def run(kind):
+        def middle(p, carry):
+            if kind == "first":
+                @pl.when(p % GROUP == 0)
+                def _():
+                    sort_group(p // GROUP)
+
+            advance(p, kind)
+            if kind == "near":
+                @pl.when(forward)
+                def _():
+                    send_on(p).start()
+
+                @pl.when(p % GROUP == GROUP - 1)
+                def _():
+                    store_grad(local(p) // GROUP).start()
+            else:
+                send_on(p).start()
+            return carry
+
+        def head(ps):
+            for p in ps:
+                advance(p, kind)
+                pass_on(p, kind)
+
+        if kind != "first":
+            @pl.when(jnp.logical_not(early))
+            def _():
+                head(range(EARLY))
+
+            head(range(EARLY, EDGE))
+            if kind == "near":
+                @pl.when(jnp.logical_not(early))
+                def _():
+                    store_grad(local(0) // GROUP).start()
+
+        lax.fori_loop(EDGE, tiles - EDGE, middle, 0)
+        if kind == "first":
+            sort_group(groups - 1)
+        head(range(tiles - EDGE, last))
+
+    @pl.when(first)
+    def _():
+        run("first")
+
+    @pl.when(nearby)
+    def _():
+        run("near")
+
+    @pl.when(jnp.logical_not(jnp.logical_or(first, nearby)))
+    def _():
+        run("plain")
 
     @pl.when(has_post)
     def _():
@@ -382,8 +424,16 @@
 
     @pl.when(jnp.logical_not(late))
     def _():
-        own_tile(local(last))
-        own_tile(local(last + 1))
+        @pl.when(nearby)
+        def _():
+            for u in range(REACH):
+                own_tile(local(last + u))
+                gradient(local(last + u), u)
+
+        @pl.when(jnp.logical_not(nearby))
+        def _():
+            for u in range(REACH):
+                own_tile(local(last + u))
 
         @pl.when(ahead_post)
         def _():
@@ -392,30 +442,42 @@
             for p in range(tiles - EDGE, tiles):
                 send_on(p).start()
 
-        @pl.when(jnp.logical_not(ahead_post))
-        def _():
-            pass_on(last)
-            pass_on(last + 1)
-
-    store_env.start()
+        @pl.when(jnp.logical_and(first, has_post))
+        def _():
+            send_post(held(last), last, col - 1, 0).start()
+            send_post(held(last + 1), last + 1, col - 1, 0).start()
+
+        @pl.when(jnp.logical_and(forward, jnp.logical_not(ahead_post)))
+        def _():
+            send_on(last).start()
+            send_on(last + 1).start()
+
+    @pl.when(nearby)
+    def _():
+        store_env.start()
 
     @pl.when(jnp.logical_not(nearby))
     def _():
         def four(i, carry):
             for u in range(GROUP):
                 gradient(GROUP * i + u, u)
-            store_grad(i).start()
             return carry
 
         lax.fori_loop(0, groups, four, 0)
 
-    @pl.when(nearby)
+    @pl.when(jnp.logical_and(nearby, early))
     def _():
         for u in range(EARLY):
             gradient(local(u), u)
         store_grad(local(0) // GROUP).start()
+
+    @pl.when(jnp.logical_and(nearby, late))
+    def _():
         for u in range(REACH):
             gradient(local(last + u), u)
+
+    @pl.when(nearby)
+    def _():
         store_grad(local(last) // GROUP).start()
 
     @pl.when(col > 0)
@@ -443,6 +505,17 @@
             send_post(held(tiles - 1 - u), tiles - 1 - u, col - 1, 0).wait_send()
 
     first_edges(lambda copy: copy.wait_send())
+
+    @pl.when(jnp.logical_not(nearby))
+    def _():
+        store_env.start()
+
+        def store(i, carry):
+            store_grad(i).start()
+            return carry
+
+        lax.fori_loop(0, groups, store, 0)
+
     store_env.wait()
 
     def stored(i, carry):

time: 78.1 us -> 77.2 us (0.988)
  Pallas kernels: 74.3 us -> 73.5 us
    pallas_call x1, Pallas kernels: 74.3 us -> 73.5 us  [per_device(): pl.pallas_call(functools.partial(sweep_kernel, ncol, nsec, pairs), out_sh...]
where the time goes in v9:
time: 77.2 us; the launch traced here: 77.1 us
  Pallas kernels  73.5 us (95%)
  local copies, waits for them, and re-layouts  2.99 us (4%)
    pallas_call x1, Pallas kernels, per_device(): pl.pallas_call(functools.partial(sweep_kernel, ncol, nsec, pairs), out_sh...  73.5 us
    unnamed x2, local copies, waits for them, and re-layouts  2.99 us

profile of v9, /device:TPU:24, one launch (start us, length us, event | category | flops | bytes accessed | tf_op | source)
XLA Modules:
  0.0 77.1 jit_solution(6357815481300291029)
XLA Ops:
  0.6 73.5 %sweep.1 = (bf16[32,128,128]{2,1,0:T(8,128)(2,1)S(1)}, bf16[16384,128]{1,0:T(8,128)(2,1)S(1)}) custom-call(s32[4,32]{1,0:T(4,128)} %bitcast.13, bf16[4096,128]{1,0:T(8,128)(2,1)} %bitcast.11, bf16[16384,128]{1,0:T(8,128)(2,1)} %bitcast.10, bf16[4096,128]{1,0:T(8,128)(2,1)} %bitcast.12), custom_call_target="tpu_custom_call" | custom-call | tf_op jit(solution)/shard_map/sweep/pallas_call | solution.py:542
  74.1 1.0 %copy.8 = bf16[1,1,4096,128]{3,2,1,0:T(8,128)(2,1)} copy(bf16[1,1,4096,128]{3,2,1,0:T(8,128)(2,1)S(1)} %bitcast.9) | data formatting | bytes 2097152
  75.1 2.0 %copy.9 = bf16[1,1,4096,4,128]{4,3,2,1,0:T(4,128)(2,1)} copy(bf16[1,1,4096,4,128]{4,3,2,1,0:T(4,128)(2,1)S(1)} %bitcast.8) | data formatting | bytes 8388608

commit v10 on v9

--- a/solution.py
+++ b/solution.py
@@ -388,7 +388,12 @@
         lax.fori_loop(EDGE, tiles - EDGE, middle, 0)
         if kind == "first":
             sort_group(groups - 1)
-        head(range(tiles - EDGE, last))
+        if kind == "near":
+            @pl.when(forward)
+            def _():
+                head(range(tiles - EDGE, last))
+        else:
+            head(range(tiles - EDGE, last))
 
     @pl.when(first)
     def _():
@@ -401,6 +406,11 @@
     @pl.when(jnp.logical_not(jnp.logical_or(first, nearby)))
     def _():
         run("plain")
+
+    @pl.when(col == 0)
+    def _():
+        arrive(last)
+        arrive(last + 1)
 
     @pl.when(has_post)
     def _():
@@ -424,7 +434,13 @@
 
     @pl.when(jnp.logical_not(late))
     def _():
-        @pl.when(nearby)
+        @pl.when(col == 0)
+        def _():
+            for u in range(EDGE):
+                own_tile(local(tiles - EDGE + u))
+                gradient(local(tiles - EDGE + u), u)
+
+        @pl.when(col == 1)
         def _():
             for u in range(REACH):
                 own_tile(local(last + u))

time: 77.2 us -> 77 us (level)
  no operation moved by 1% of the time
where the time goes in v10:
time: 77 us; the launch traced here: 76.9 us
  Pallas kernels  73.3 us (95%)
  local copies, waits for them, and re-layouts  2.99 us (4%)
    pallas_call x1, Pallas kernels, per_device(): pl.pallas_call(functools.partial(sweep_kernel, ncol, nsec, pairs), out_sh...  73.3 us
    unnamed x2, local copies, waits for them, and re-layouts  2.99 us

profile of v10, /device:TPU:24, one launch (start us, length us, event | category | flops | bytes accessed | tf_op | source)
XLA Modules:
  0.0 76.9 jit_solution(9173452839608331584)
XLA Ops:
  0.6 73.3 %sweep.1 = (bf16[32,128,128]{2,1,0:T(8,128)(2,1)S(1)}, bf16[16384,128]{1,0:T(8,128)(2,1)S(1)}) custom-call(s32[4,32]{1,0:T(4,128)} %bitcast.13, bf16[4096,128]{1,0:T(8,128)(2,1)} %bitcast.11, bf16[16384,128]{1,0:T(8,128)(2,1)} %bitcast.10, bf16[4096,128]{1,0:T(8,128)(2,1)} %bitcast.12), custom_call_target="tpu_custom_call" | custom-call | tf_op jit(solution)/shard_map/sweep/pallas_call | solution.py:558
  73.9 1.0 %copy.8 = bf16[1,1,4096,128]{3,2,1,0:T(8,128)(2,1)} copy(bf16[1,1,4096,128]{3,2,1,0:T(8,128)(2,1)S(1)} %bitcast.9) | data formatting | bytes 2097152
  74.9 2.0 %copy.9 = bf16[1,1,4096,4,128]{4,3,2,1,0:T(4,128)(2,1)} copy(bf16[1,1,4096,4,128]{4,3,2,1,0:T(4,128)(2,1)S(1)} %bitcast.8) | data formatting | bytes 8388608
